TPU v7x, 32 devices: a whole 2x2x4 slice. The times are simulated.
32 devices in a mesh: dp: 8 (over y, x, core), mp: 4 (over z).
Axes of the slice: x: 2, y: 2, z: 4, core: 2. Of those that a mesh axis runs over, the one named last changes fastest.
Arguments:
- queries: bfloat16 [2048, 2048], P('dp', 'mp'), may hold values from -24 to 24
- context_grad: bfloat16 [2048, 2048], P('dp', 'mp'), may hold values from -6 to 6
- encoder_rows: bfloat16 [7168, 4096], P('dp'), may hold values from -60 to 60
- key_weight: bfloat16 [4096, 2048], P('dp', 'mp'), may hold values from -1 to 1
- value_weight: bfloat16 [4096, 2048], P('dp', 'mp'), may hold values from -0.09375 to 0.09375
- document_lengths: int32 [8, 4], P('dp'), may hold values from 1 to 128, 256 in all within a row
- block_bin: int32 [56], P('dp'), may hold values from 0 to 7, as said below
- block_document: int32 [56], P('dp'), may hold values from 0 to 3
Outputs:
- context: bfloat16 [2048, 2048], P('dp', 'mp')
- query_grad: bfloat16 [2048, 2048], P('dp', 'mp')
- encoder_grad: bfloat16 [7168, 4096], P('dp', 'mp')
- key_weight_grad: bfloat16 [4096, 2048], P('dp', 'mp')
- value_weight_grad: bfloat16 [4096, 2048], P('dp', 'mp')
Inputs may be any that keep to these rules, and one draw needn't show every extreme that they name: `block_bin`: each index of dp holds 7 encoder blocks and sends them to 7 different bins; one bin receives a block from every index of dp.
All inputs are finite; a program needn't handle non-finite values.
Results may differ from a plain program's by a relative error of at most 0.03.
The roundings to bfloat16 on the way count: a program that leaves them out, or rounds other values in their place, can miss the bound.
Values may be sent and summed in bfloat16 or wider, within the bound.
A program may use at most 128 MiB of HBM per device.

v0:
```python
import functools

import jax
import jax.numpy as jnp
from jax import lax
from jax.experimental import pallas as pl
from jax.experimental.pallas import tpu as pltpu
from jax.sharding import PartitionSpec as P

HD = 256
BLK = 128


masked_value = -1e30


def attend_weights(scores, live_mask):
    present = jnp.any(live_mask, axis=1)[None, :, None]
    blocked = jnp.where(live_mask[None], scores, masked_value)
    highest = jnp.max(blocked, axis=2, keepdims=True)
    highest = jnp.where(present, highest, 0.0)
    raised = jnp.exp(jnp.where(live_mask[None], scores - highest, masked_value))
    totals = jnp.maximum(jnp.sum(raised, axis=2, keepdims=True), 1.0)
    return raised / totals


def token_documents(lengths, token_count):
    doc_ends = jnp.cumsum(lengths)
    positions = jnp.arange(token_count, dtype=jnp.int32)
    return jnp.sum((doc_ends[None, :] <= positions[:, None]).astype(jnp.int32), axis=1)


def per_device(
    queries,
    context_grad,
    encoder_rows,
    key_weight,
    value_weight,
    document_lengths,
    block_bin,
    block_document,
):
    bin_count = lax.axis_size("dp")
    full_key, full_value = (
        lax.all_gather(key_weight, "dp", axis=0, tiled=True),
        lax.all_gather(value_weight, "dp", axis=0, tiled=True),
    )
    head_width = full_key.shape[1]
    head_count = head_width // HD
    block_rows = BLK
    blocks_here = block_bin.shape[0]
    both_weights = jnp.concatenate([full_key, full_value], axis=1)
    projected = jnp.dot(encoder_rows, both_weights, preferred_element_type=jnp.float32).astype(
        jnp.bfloat16
    )
    route_table = (block_bin[:, None] == jnp.arange(bin_count, dtype=jnp.int32)[None, :]).astype(
        jnp.bfloat16
    )
    flat_blocks = projected.reshape(blocks_here, block_rows * 2 * head_width)
    outbound = lax.dot_general(
        route_table, flat_blocks, (((0,), (0,)), ((), ())), preferred_element_type=jnp.float32
    )
    outbound = outbound.astype(jnp.bfloat16).reshape(bin_count, block_rows, 2 * head_width)
    slot_docs = (
        lax.dot_general(
            route_table.astype(jnp.float32),
            (block_document + 1).astype(jnp.float32),
            (((0,), (0,)), ((), ())),
        )
        - 1.0
    )
    tag_rows = jnp.broadcast_to(slot_docs[:, None], (bin_count, block_rows)).astype(jnp.bfloat16)
    arrived, arrived_tags = (
        lax.all_to_all(outbound, "dp", split_axis=0, concat_axis=0, tiled=True),
        lax.all_to_all(tag_rows, "dp", split_axis=0, concat_axis=0, tiled=True),
    )
    key_slots = arrived[:, :, :head_width].reshape(bin_count * block_rows, head_count, HD)
    value_slots = arrived[:, :, head_width:].reshape(bin_count * block_rows, head_count, HD)
    token_count = queries.shape[0]
    token_docs = token_documents(document_lengths[0], token_count).astype(jnp.float32)
    live_mask = arrived_tags.reshape(-1).astype(jnp.float32)[None, :] == token_docs[:, None]
    query_heads = queries.reshape(token_count, head_count, HD)
    grad_heads = context_grad.reshape(token_count, head_count, HD)
    scaling = HD ** (-0.5)
    scores = (
        jnp.einsum("thd,shd->hts", query_heads, key_slots, preferred_element_type=jnp.float32)
        * scaling
    )
    attention = attend_weights(scores, live_mask)
    rounded = attention.astype(jnp.bfloat16)
    context = jnp.einsum(
        "hts,shd->thd", rounded, value_slots, preferred_element_type=jnp.float32
    ).astype(jnp.bfloat16)
    grad_raw = jnp.einsum(
        "thd,shd->hts", grad_heads, value_slots, preferred_element_type=jnp.float32
    )
    deltas = jnp.sum(attention * grad_raw, axis=2, keepdims=True)
    score_grad = (attention * (grad_raw - deltas) * scaling).astype(jnp.bfloat16)
    query_grad = jnp.einsum(
        "hts,shd->thd", score_grad, key_slots, preferred_element_type=jnp.float32
    ).astype(jnp.bfloat16)
    key_grad = jnp.einsum(
        "hts,thd->shd", score_grad, query_heads, preferred_element_type=jnp.float32
    ).astype(jnp.bfloat16)
    value_grad = jnp.einsum(
        "hts,thd->shd", rounded, grad_heads, preferred_element_type=jnp.float32
    ).astype(jnp.bfloat16)
    slot_grads = jnp.concatenate(
        [
            key_grad.reshape(bin_count, block_rows, head_width),
            value_grad.reshape(bin_count, block_rows, head_width),
        ],
        axis=2,
    )
    returned = lax.all_to_all(slot_grads, "dp", split_axis=0, concat_axis=0, tiled=True)
    own_grads = jnp.dot(
        route_table,
        returned.reshape(bin_count, block_rows * 2 * head_width),
        preferred_element_type=jnp.float32,
    )
    own_grads = own_grads.astype(jnp.bfloat16).reshape(encoder_rows.shape[0], 2 * head_width)
    weight_terms = lax.dot_general(
        encoder_rows, own_grads, (((0,), (0,)), ((), ())), preferred_element_type=jnp.float32
    )
    weight_sums = lax.psum_scatter(
        weight_terms.astype(jnp.bfloat16), "dp", scatter_dimension=0, tiled=True
    ).astype(jnp.float32)
    key_weight_grad = weight_sums[:, :head_width].astype(jnp.bfloat16)
    value_weight_grad = weight_sums[:, head_width:].astype(jnp.bfloat16)
    row_terms = lax.dot_general(
        own_grads, both_weights, (((1,), (1,)), ((), ())), preferred_element_type=jnp.float32
    )
    encoder_grad = lax.psum_scatter(
        row_terms.astype(jnp.bfloat16), "mp", scatter_dimension=1, tiled=True
    )
    return (
        context.reshape(token_count, head_width),
        query_grad.reshape(token_count, head_width),
        encoder_grad,
        key_weight_grad,
        value_weight_grad,
    )


MESH = pl.DeviceIdType.MESH


def contract(a, b, dim_a, dim_b):
    return lax.dot_general(
        a, b, (((dim_a,), (dim_b,)), ((), ())), preferred_element_type=jnp.float32
    )


def front_kernel(
    n,
    q_ref,
    g_ref,
    enc_hbm,
    kw_ref,
    vw_ref,
    tags_ref,
    routes_ref,
    token_doc_ref,
    ctx_ref,
    qg_ref,
    back_hbm,
    wfull_hbm,
    enc,
    wts,
    acc,
    outbound,
    arrived,
    arrived_tags,
    grads,
    ret,
    local_sem,
    gather_send,
    gather_recv,
    tag_send,
    tag_recv,
    out_send,
    out_recv,
    back_send,
    back_recv,
):
    me = lax.axis_index("dp")
    core = me % 2
    x = (me // 2) % 2
    y = me // 4

    def place(py, px, pc):
        return (py * 2 + px) * 2 + pc

    at_x, at_y = place(y, 1 - x, core), place(1 - y, x, core)
    at_c, at_d = place(y, x, 1 - core), place(1 - y, 1 - x, core)
    c_x, c_y = place(y, 1 - x, 1 - core), place(1 - y, x, 1 - core)
    c_d = place(1 - y, 1 - x, 1 - core)
    depth, width = kw_ref.shape
    rows = enc.shape[0]
    slots = n
    blk = BLK

    load_enc = pltpu.make_async_copy(enc_hbm, enc, local_sem.at[0])
    load_enc.start()
    barrier = pltpu.get_barrier_semaphore()
    for d in range(1, n):
        pl.semaphore_signal(
            barrier, inc=1, device_id={"dp": (me + d) % n}, device_id_type=MESH
        )
    pl.semaphore_wait(barrier, n - 1)

    def land(src, part):
        return wts.at[src, :, pl.ds(part * width, width)]

    started = []

    def ship(ident, ref, src, part, to):
        copy = pltpu.make_async_remote_copy(
            src_ref=ref,
            dst_ref=land(src, part),
            send_sem=gather_send.at[ident],
            recv_sem=gather_recv.at[ident],
            device_id={"dp": to},
            device_id_type=MESH,
        )
        copy.start()
        started.append(copy)

    def landed(ident, src, part):
        pltpu.make_async_remote_copy(
            src_ref=land(src, part),
            dst_ref=land(src, part),
            send_sem=gather_send.at[ident],
            recv_sem=gather_recv.at[ident],
            device_id={"dp": at_c},
            device_id_type=MESH,
        ).wait_recv()

    ship(0, kw_ref, me, 0, at_x)
    ship(3, vw_ref, me, 1, at_y)
    ship(1, vw_ref, me, 1, at_x)
    ship(2, kw_ref, me, 0, at_y)
    ship(6, kw_ref, me, 0, at_c)
    ship(7, vw_ref, me, 1, at_c)
    own_k = pltpu.make_async_copy(kw_ref, land(me, 0), local_sem.at[1])
    own_v = pltpu.make_async_copy(vw_ref, land(me, 1), local_sem.at[2])
    own_k.start()
    own_v.start()
    tag_copies = []
    for d in range(1, n):
        to = (me + d) % n
        copy = pltpu.make_async_remote_copy(
            src_ref=tags_ref.at[to],
            dst_ref=arrived_tags.at[me],
            send_sem=tag_send.at[d],
            recv_sem=tag_recv.at[d],
            device_id={"dp": to},
            device_id_type=MESH,
        )
        copy.start()
        tag_copies.append(copy)
    arrived_tags[me] = tags_ref[me]
    own_k.wait()
    own_v.wait()
    load_enc.wait()

    tile = rows // 2

    def multiply(src, part, first=False):
        columns = pl.ds(pl.multiple_of(src * depth, depth), depth)
        cols = pl.ds(part * width, width)

        @pl.loop(0, 2)
        def _(t):
            r = pl.ds(pl.multiple_of(t * tile, tile), tile)
            product = jnp.dot(
                enc[r, columns], wts[src, :, cols], preferred_element_type=jnp.float32
            )
            if first:
                acc[r, cols] = product
            else:
                acc[r, cols] += product

    multiply(me, 0, True)
    multiply(me, 1, True)
    landed(6, at_c, 0)
    multiply(at_c, 0)
    landed(7, at_c, 1)
    multiply(at_c, 1)
    landed(0, at_x, 0)
    ship(4, land(at_x, 0), at_x, 0, at_y)
    ship(8, land(at_x, 0), at_x, 0, at_c)
    landed(3, at_y, 1)
    ship(5, land(at_y, 1), at_y, 1, at_x)
    ship(11, land(at_y, 1), at_y, 1, at_c)
    multiply(at_x, 0)
    multiply(at_y, 1)
    landed(8, c_x, 0)
    multiply(c_x, 0)
    landed(11, c_y, 1)
    multiply(c_y, 1)
    landed(1, at_x, 1)
    ship(9, land(at_x, 1), at_x, 1, at_c)
    landed(2, at_y, 0)
    ship(10, land(at_y, 0), at_y, 0, at_c)
    multiply(at_x, 1)
    multiply(at_y, 0)
    landed(9, c_x, 1)
    multiply(c_x, 1)
    landed(10, c_y, 0)
    multiply(c_y, 0)
    landed(4, at_d, 0)
    ship(12, land(at_d, 0), at_d, 0, at_c)
    landed(5, at_d, 1)
    ship(13, land(at_d, 1), at_d, 1, at_c)
    multiply(at_d, 0)
    multiply(at_d, 1)
    landed(12, c_d, 0)
    multiply(c_d, 0)
    landed(13, c_d, 1)
    multiply(c_d, 1)
    keep = pltpu.make_async_copy(wts, wfull_hbm, local_sem.at[3])
    keep.start()

    out_copies = []
    mine = pl.ds(pl.multiple_of(me * blk, blk), blk)
    for d in [*range(1, n), 0]:
        to = (me + d) % n

        @pl.loop(0, blk // 16)
        def _(t):
            picked = jnp.zeros((16, 2 * width), jnp.float32)
            for b in range(rows // blk):
                row = routes_ref[to, b : b + 1, :]
                wide = jnp.concatenate([row] * (2 * width // BLK), axis=1) > 0.5
                part = acc[pl.ds(pl.multiple_of(b * blk + t * 16, 16), 16), :]
                picked = jnp.where(wide, part, picked)
            outbound[to, pl.ds(pl.multiple_of(t * 16, 16), 16), :] = picked.astype(jnp.bfloat16)

        if d == 0:
            arrived[mine, :] = outbound[to]
            continue
        copy = pltpu.make_async_remote_copy(
            src_ref=outbound.at[to],
            dst_ref=arrived.at[mine, :],
            send_sem=out_send.at[d],
            recv_sem=out_recv.at[d],
            device_id={"dp": to},
            device_id_type=MESH,
        )
        copy.start()
        out_copies.append(copy)

    token_doc = token_doc_ref[:, 0:1]
    for copy in tag_copies:
        copy.wait()
    for copy in out_copies:
        copy.wait()
    tag_row = jnp.concatenate([arrived_tags[s, 0:1, :] for s in range(slots)], axis=1)
    live = tag_row == token_doc
    present = jnp.max(jnp.where(live, 1.0, 0.0), axis=1, keepdims=True) > 0.0
    scaling = HD ** (-0.5)
    back_copies = []
    for h in range(width // HD):
        hk, hv = pl.ds(h * HD, HD), pl.ds(width + h * HD, HD)
        q, g = q_ref[:, hk], g_ref[:, hk]
        scores = contract(q, arrived[:, hk], 1, 1) * scaling
        highest = jnp.max(jnp.where(live, scores, masked_value), axis=1, keepdims=True)
        highest = jnp.where(present, highest, 0.0)
        raised = jnp.exp(jnp.where(live, scores - highest, masked_value))
        totals = jnp.maximum(jnp.sum(raised, axis=1, keepdims=True), 1.0)
        attention = raised / totals
        rounded = attention.astype(jnp.bfloat16)
        grad_raw = contract(g, arrived[:, hv], 1, 1)
        deltas = jnp.sum(attention * grad_raw, axis=1, keepdims=True)
        score_grad = (attention * (grad_raw - deltas) * scaling).astype(jnp.bfloat16)
        grads[h, 0] = contract(score_grad, q, 0, 0).astype(jnp.bfloat16)
        grads[h, 1] = contract(rounded, g, 0, 0).astype(jnp.bfloat16)
        for d in range(1, n):
            to = (me + d) % n
            copy = pltpu.make_async_remote_copy(
                src_ref=grads.at[h, :, pl.ds(pl.multiple_of(to * blk, blk), blk), :],
                dst_ref=ret.at[h, :, pl.ds(pl.multiple_of(me * blk, blk), blk), :],
                send_sem=back_send.at[h, d],
                recv_sem=back_recv.at[h, d],
                device_id={"dp": to},
                device_id_type=MESH,
            )
            copy.start()
            back_copies.append(copy)
        ret[h, :, mine, :] = grads[h, :, mine, :]
        ctx_ref[:, hk] = jnp.dot(
            rounded, arrived[:, hv], preferred_element_type=jnp.float32
        ).astype(jnp.bfloat16)
        qg_ref[:, hk] = jnp.dot(
            score_grad, arrived[:, hk], preferred_element_type=jnp.float32
        ).astype(jnp.bfloat16)
    for copy in started:
        copy.wait_send()
    keep.wait()
    for copy in back_copies:
        copy.wait()
    put = pltpu.make_async_copy(ret, back_hbm, local_sem.at[0])
    put.start()
    put.wait()


def pick_kernel(bins_ref, back_ref, own_ref):
    heads = back_ref.shape[0]
    for h in range(heads):
        own_ref[:, pl.ds(h * HD, HD)] = back_ref[h, 0]
        own_ref[:, pl.ds((heads + h) * HD, HD)] = back_ref[h, 1]


def pick_blocks(back, bins):
    heads = back.shape[0]
    count = bins.shape[0]
    return pl.pallas_call(
        pick_kernel,
        out_shape=jax.ShapeDtypeStruct((count * BLK, 2 * heads * HD), back.dtype),
        grid_spec=pltpu.PrefetchScalarGridSpec(
            num_scalar_prefetch=1,
            grid=(count,),
            in_specs=[pl.BlockSpec((heads, 2, BLK, HD), lambda b, bins: (0, 0, bins[b], 0))],
            out_specs=pl.BlockSpec((BLK, 2 * heads * HD), lambda b, bins: (b, 0)),
        ),
    )(bins, back)


def front(n, queries, context_grad, encoder_rows, key_weight, value_weight, lengths, bins, docs):
    rows, model = encoder_rows.shape
    depth, width = key_weight.shape
    heads = width // HD
    tokens = queries.shape[0]
    hits = bins[:, None] == jnp.arange(n, dtype=jnp.int32)[None, :]
    slot_docs = jnp.sum(jnp.where(hits, docs[:, None] + 1, 0), axis=0) - 1
    tags = jnp.broadcast_to(slot_docs.astype(jnp.float32)[:, None, None], (n, 8, BLK))
    padded = jnp.pad(hits.astype(jnp.float32).T, ((0, 0), (0, -bins.shape[0] % 8)))
    routes = jnp.broadcast_to(padded[:, :, None], (n, padded.shape[1], BLK))
    position = lax.broadcasted_iota(jnp.int32, (tokens, BLK), 0)
    token_doc = jnp.zeros((tokens, BLK), jnp.float32)
    end = jnp.int32(0)
    for k in range(lengths.shape[1]):
        end = end + lengths[0, k]
        token_doc = token_doc + jnp.where(position >= end, 1.0, 0.0)
    vmem = pl.BlockSpec(memory_space=pltpu.VMEM)
    hbm = pl.BlockSpec(memory_space=pl.ANY)
    bf16 = jnp.bfloat16
    dma = pltpu.SemaphoreType.DMA
    return pl.pallas_call(
        functools.partial(front_kernel, n),
        out_shape=(
            jax.ShapeDtypeStruct((tokens, width), bf16),
            jax.ShapeDtypeStruct((tokens, width), bf16),
            jax.ShapeDtypeStruct((heads, 2, n * BLK, HD), bf16),
            jax.ShapeDtypeStruct((n, depth, 2 * width), bf16),
        ),
        in_specs=[vmem, vmem, hbm, vmem, vmem, vmem, vmem, vmem],
        out_specs=(vmem, vmem, hbm, hbm),
        scratch_shapes=[
            pltpu.VMEM((rows, model), bf16),
            pltpu.VMEM((n, depth, 2 * width), bf16),
            pltpu.VMEM((rows, 2 * width), jnp.float32),
            pltpu.VMEM((n, BLK, 2 * width), bf16),
            pltpu.VMEM((n * BLK, 2 * width), bf16),
            pltpu.VMEM((n, 8, BLK), jnp.float32),
            pltpu.VMEM((heads, 2, n * BLK, HD), bf16),
            pltpu.VMEM((heads, 2, n * BLK, HD), bf16),
            dma((4,)),
            dma((14,)),
            dma((14,)),
            dma((n,)),
            dma((n,)),
            dma((n,)),
            dma((n,)),
            dma((heads, n)),
            dma((heads, n)),
        ],
        compiler_params=pltpu.CompilerParams(
            collective_id=0, has_side_effects=True, vmem_limit_bytes=62 * 1024 * 1024
        ),
    )(
        queries,
        context_grad,
        encoder_rows,
        key_weight,
        value_weight,
        tags,
        routes,
        token_doc,
    )


def line_kernel(
    count, own_ref, weights_hbm, out_ref, weights, got, sent, total, load_sem, send_sem, recv_sem
):
    z = lax.axis_index("mp")
    chunks = own_ref.shape[0] // BLK
    right, left = (z + 1) % count, (z + count - 1) % count
    loads = [
        pltpu.make_async_copy(weights_hbm.at[d], weights.at[d], load_sem.at[d])
        for d in range(count)
    ]
    for load in loads:
        load.start()
    barrier = pltpu.get_barrier_semaphore()
    for d in range(1, count):
        pl.semaphore_signal(
            barrier, inc=1, device_id={"mp": (z + d) % count}, device_id_type=MESH
        )
    pl.semaphore_wait(barrier, count - 1)
    for load in loads:
        load.wait()

    def link(way, dest, r):
        return pltpu.make_async_remote_copy(
            src_ref=sent.at[way, dest, r],
            dst_ref=got.at[way, dest, r],
            send_sem=send_sem.at[way, dest, r],
            recv_sem=recv_sem.at[way, dest, r],
            device_id={"mp": left if way else right},
            device_id_type=MESH,
        )

    def rows(r):
        return pl.ds(pl.multiple_of(r * BLK, BLK), BLK)

    def pass_on(way, dest, r):
        first = z == (count - 1 if way else 0)
        total[...] = contract(own_ref[rows(r), :], weights[dest], 1, 1)

        @pl.when(first)
        def _():
            sent[way, dest, r] = total[...].astype(jnp.bfloat16)

        @pl.when(jnp.logical_not(first))
        def _():
            link(way, dest, r).wait_recv()
            added = total[...] + got[way, dest, r].astype(jnp.float32)
            sent[way, dest, r] = added.astype(jnp.bfloat16)

        link(way, dest, r).start()

    for phase in range(count - 1):

        @pl.loop(0, chunks)
        def _(r):
            @pl.when(z < count - 1 - phase)
            def _():
                pass_on(0, count - 1 - phase, r)

            @pl.when(z > phase)
            def _():
                pass_on(1, phase, r)

    @pl.loop(0, chunks)
    def _(r):
        total[...] = contract(own_ref[rows(r), :], weights[z], 1, 1)

        @pl.when(z > 0)
        def _():
            link(0, z, r).wait_recv()
            total[...] += got[0, z, r].astype(jnp.float32)

        @pl.when(z < count - 1)
        def _():
            link(1, z, r).wait_recv()
            total[...] += got[1, z, r].astype(jnp.float32)

        out_ref[rows(r), :] = total[...].astype(jnp.bfloat16)

    for phase in range(count - 1):

        @pl.loop(0, chunks)
        def _(r):
            @pl.when(z < count - 1 - phase)
            def _():
                link(0, count - 1 - phase, r).wait_send()

            @pl.when(z > phase)
            def _():
                link(1, phase, r).wait_send()


def line_sum(own, weights, count):
    rows, width = own.shape
    out_width = weights.shape[0] // count
    chunks = rows // BLK
    vmem = pl.BlockSpec(memory_space=pltpu.VMEM)
    dma = pltpu.SemaphoreType.DMA
    return pl.pallas_call(
        functools.partial(line_kernel, count),
        out_shape=jax.ShapeDtypeStruct((rows, out_width), own.dtype),
        in_specs=[vmem, pl.BlockSpec(memory_space=pl.ANY)],
        out_specs=vmem,
        scratch_shapes=[
            pltpu.VMEM((count, out_width, width), own.dtype),
            pltpu.VMEM((2, count, chunks, BLK, out_width), own.dtype),
            pltpu.VMEM((2, count, chunks, BLK, out_width), own.dtype),
            pltpu.VMEM((BLK, out_width), jnp.float32),
            dma((count,)),
            dma((2, count, chunks)),
            dma((2, count, chunks)),
        ],
        compiler_params=pltpu.CompilerParams(
            collective_id=1, has_side_effects=True, vmem_limit_bytes=58 * 1024 * 1024
        ),
        cost_estimate=pl.CostEstimate(
            flops=2 * rows * width * out_width * count,
            bytes_accessed=300 * 1024 * 1024,
            transcendentals=0,
        ),
    )(own, weights.reshape(count, out_width, width))


def per_device_cube(
    queries,
    context_grad,
    encoder_rows,
    key_weight,
    value_weight,
    document_lengths,
    block_bin,
    block_document,
):
    n, count = lax.axis_size("dp"), lax.axis_size("mp")
    width = key_weight.shape[1]
    context, query_grad, back, weights = front(
        n,
        queries,
        context_grad,
        encoder_rows,
        key_weight,
        value_weight,
        document_lengths,
        block_bin,
        block_document,
    )
    weights = weights.reshape(-1, 2 * width)
    own = pick_blocks(back, block_bin)
    weight_terms = contract(encoder_rows, own, 0, 0)
    weight_sums = lax.psum_scatter(
        weight_terms.astype(jnp.bfloat16), "dp", scatter_dimension=0, tiled=True
    )
    encoder_grad = line_sum(own, weights, count)
    return context, query_grad, encoder_grad, weight_sums[:, :width], weight_sums[:, width:]


def solution(mesh):
    in_specs = (
        P("dp", "mp"),
        P("dp", "mp"),
        P("dp", None),
        P("dp", "mp"),
        P("dp", "mp"),
        P("dp", None),
        P("dp"),
        P("dp"),
    )
    out_specs = (P("dp", "mp"), P("dp", "mp"), P("dp", "mp"), P("dp", "mp"), P("dp", "mp"))
    cube = mesh.shape["dp"] == 2 * 2 * 2
    return jax.shard_map(
        per_device_cube if cube else per_device, mesh=mesh, in_specs=in_specs, out_specs=out_specs, check_vma=False
    )
```

profile of v0, /device:TPU:10, one launch (start us, length us, event | category | flops | bytes accessed | tf_op | source)
XLA Modules:
  0.0 298.2 jit_solution(16317064060790212945)
XLA Ops:
  7.2 0.0 reduce-scatter.2.cloned.1.call-start
  7.2 0.7 broadcast_add_fusion
  7.9 0.7 iota_compare_fusion
  8.5 0.7 select_reduce_fusion
  9.3 1.4 fusion.4
  13.3 0.7 fusion.2
  13.9 0.7 broadcast_in_dim.44.routes_ref
  14.6 0.7 broadcast_in_dim.43.tags_ref
  15.3 0.8 iota.21.token_doc_ref
  16.1 93.6 %shard_map.119 = (bf16[256,512]{1,0:T(8,128)(2,1)}, bf16[256,512]{1,0:T(8,128)(2,1)}, bf16[2,2,1024,256]{3,2,1,0:T(8,128)(2,1)}, bf16[8,512,1024]{2,1,0:T(8,128)(2,1)}) custom-call(bf16[256,512]{1,0:T(8,128)(2,1)} %q_ref.1, bf16[256,512]{1,0:T(8,128)(2,1)} %g_ref.1, bf16[896,4096]{1,0:T(8,128)(2,1)} %enc_hbm.1, bf16[512,512]{1,0:T(8,128)(2,1)} %kw_ref.1, ...), custom_call_target="tpu_custom_call" | custom-call | tf_op jit(solution)/shard_map/pallas_call | solution.py:450
  109.7 5.8 %shard_map.120.own_ref = bf16[896,1024]{1,0:T(8,128)(2,1)} custom-call(s32[7]{0:T(128)} %bins_ref.1, bf16[2,2,1024,256]{3,2,1,0:T(8,128)(2,1)} %get-tuple-element.11.back_ref), custom_call_target="tpu_custom_call" | custom-call | tf_op jit(solution)/shard_map/pallas_call | solution.py:418
  115.5 13.8 %convert_bitcast_fusion = bf16[4096,1024]{0,1:T(8,128)(2,1)} fusion(bf16[896,1024]{1,0:T(8,128)(2,1)} %shard_map.120.own_ref, bf16[896,4096]{1,0:T(8,128)(2,1)} %enc_hbm.1), kind=kOutput, calls=%fused_computation | convolution fusion | flops 7520387072 | bytes 17563648 | tf_op jit(solution)/shard_map/dot_general | solution.py:149
  129.3 0.0 reduce-scatter.2.cloned.1.call-update
  129.3 0.0 copy-start.1
  129.3 0.0 copy-start
  129.3 154.4 %shard_map.121 = bf16[896,1024]{1,0:T(8,128)(2,1)} custom-call(bf16[896,1024]{1,0:T(8,128)(2,1)} %shard_map.120.own_ref, bf16[4,1024,1024]{2,1,0:T(8,128)(2,1)} %bitcast.9), custom_call_target="tpu_custom_call" | custom-call | flops 7516192768 | bytes 314572800 | tf_op jit(solution)/shard_map/pallas_call | solution.py:591
  283.8 0.0 reduce-scatter.2.cloned.1.call-done
  283.8 1.3 fusion.3
  285.1 1.0 copy.16
  286.1 1.0 copy.15
  287.1 0.0 copy-done.1
  287.1 0.7 copy.20
  287.8 0.0 copy-done
  287.8 0.7 copy.21
  288.5 2.9 copy.22
  (2 shorter events, 0.0 us)
Async XLA Ops:
  7.2 276.6 %reduce-scatter.2.cloned.1.call-start = ((), (), s32[]{:S(2)}) async-start(), calls=%async_computation.1 | async-start | bytes 9437184 | tf_op jit(solution)/shard_map/reduce_scatter | solution.py:642
  129.3 157.8 %copy-start.1 = (bf16[256,512]{1,0:T(8,128)(2,1)S(1)}, bf16[256,512]{1,0:T(8,128)(2,1)}, u32[]{:S(2)}) copy-start(bf16[256,512]{1,0:T(8,128)(2,1)} %get-tuple-element.34) | copy-start | bytes 786436
  129.3 158.5 %copy-start = (bf16[256,512]{1,0:T(8,128)(2,1)S(1)}, bf16[256,512]{1,0:T(8,128)(2,1)}, u32[]{:S(2)}) copy-start(bf16[256,512]{1,0:T(8,128)(2,1)} %get-tuple-element.35) | copy-start | bytes 786436
Sparse Core Ops, SparseCore 0:
  129.4 73.6 reduce-scatter.1
where the time goes:
time: 299 us; the launch traced here: 298 us
  Pallas kernels  254 us (85%)
  between operations  16.7 us (6%)
  matrix products  13.8 us (5%)
  local copies, waits for them, and re-layouts  11.1 us (4%)
    pallas_call x1, Pallas kernels, line_sum(): pl.pallas_call(functools.partial(line_kernel, count), out_shape=jax.Shape...  154 us
    pallas_call x1, Pallas kernels, front(): pl.pallas_call(functools.partial(front_kernel, n), out_shape=(jax.ShapeDt...  93.6 us
    dot_general x1, matrix products, contract(): lax.dot_general(a, b, (((dim_a,), (dim_b,)), ((), ())), preferred_element...  13.8 us
    unnamed x9, local copies, waits for them, and re-layouts  6.29 us
  transfers between devices with their start and end apart: 1, of which 0 were waited for; matrix products, arithmetic and copies ran while one was open for 0% of the time, Pallas kernels for 52%

commit v1 on v0

v1 whole, which is shorter than its diff:
```python
import functools

import jax
import jax.numpy as jnp
from jax import lax
from jax.experimental import pallas as pl
from jax.experimental.pallas import tpu as pltpu
from jax.sharding import PartitionSpec as P

HD = 256
BLK = 128


masked_value = -1e30


def attend_weights(scores, live_mask):
    present = jnp.any(live_mask, axis=1)[None, :, None]
    blocked = jnp.where(live_mask[None], scores, masked_value)
    highest = jnp.max(blocked, axis=2, keepdims=True)
    highest = jnp.where(present, highest, 0.0)
    raised = jnp.exp(jnp.where(live_mask[None], scores - highest, masked_value))
    totals = jnp.maximum(jnp.sum(raised, axis=2, keepdims=True), 1.0)
    return raised / totals


def token_documents(lengths, token_count):
    doc_ends = jnp.cumsum(lengths)
    positions = jnp.arange(token_count, dtype=jnp.int32)
    return jnp.sum((doc_ends[None, :] <= positions[:, None]).astype(jnp.int32), axis=1)


def per_device(
    queries,
    context_grad,
    encoder_rows,
    key_weight,
    value_weight,
    document_lengths,
    block_bin,
    block_document,
):
    bin_count = lax.axis_size("dp")
    full_key, full_value = (
        lax.all_gather(key_weight, "dp", axis=0, tiled=True),
        lax.all_gather(value_weight, "dp", axis=0, tiled=True),
    )
    head_width = full_key.shape[1]
    head_count = head_width // HD
    block_rows = BLK
    blocks_here = block_bin.shape[0]
    both_weights = jnp.concatenate([full_key, full_value], axis=1)
    projected = jnp.dot(encoder_rows, both_weights, preferred_element_type=jnp.float32).astype(
        jnp.bfloat16
    )
    route_table = (block_bin[:, None] == jnp.arange(bin_count, dtype=jnp.int32)[None, :]).astype(
        jnp.bfloat16
    )
    flat_blocks = projected.reshape(blocks_here, block_rows * 2 * head_width)
    outbound = lax.dot_general(
        route_table, flat_blocks, (((0,), (0,)), ((), ())), preferred_element_type=jnp.float32
    )
    outbound = outbound.astype(jnp.bfloat16).reshape(bin_count, block_rows, 2 * head_width)
    slot_docs = (
        lax.dot_general(
            route_table.astype(jnp.float32),
            (block_document + 1).astype(jnp.float32),
            (((0,), (0,)), ((), ())),
        )
        - 1.0
    )
    tag_rows = jnp.broadcast_to(slot_docs[:, None], (bin_count, block_rows)).astype(jnp.bfloat16)
    arrived, arrived_tags = (
        lax.all_to_all(outbound, "dp", split_axis=0, concat_axis=0, tiled=True),
        lax.all_to_all(tag_rows, "dp", split_axis=0, concat_axis=0, tiled=True),
    )
    key_slots = arrived[:, :, :head_width].reshape(bin_count * block_rows, head_count, HD)
    value_slots = arrived[:, :, head_width:].reshape(bin_count * block_rows, head_count, HD)
    token_count = queries.shape[0]
    token_docs = token_documents(document_lengths[0], token_count).astype(jnp.float32)
    live_mask = arrived_tags.reshape(-1).astype(jnp.float32)[None, :] == token_docs[:, None]
    query_heads = queries.reshape(token_count, head_count, HD)
    grad_heads = context_grad.reshape(token_count, head_count, HD)
    scaling = HD ** (-0.5)
    scores = (
        jnp.einsum("thd,shd->hts", query_heads, key_slots, preferred_element_type=jnp.float32)
        * scaling
    )
    attention = attend_weights(scores, live_mask)
    rounded = attention.astype(jnp.bfloat16)
    context = jnp.einsum(
        "hts,shd->thd", rounded, value_slots, preferred_element_type=jnp.float32
    ).astype(jnp.bfloat16)
    grad_raw = jnp.einsum(
        "thd,shd->hts", grad_heads, value_slots, preferred_element_type=jnp.float32
    )
    deltas = jnp.sum(attention * grad_raw, axis=2, keepdims=True)
    score_grad = (attention * (grad_raw - deltas) * scaling).astype(jnp.bfloat16)
    query_grad = jnp.einsum(
        "hts,shd->thd", score_grad, key_slots, preferred_element_type=jnp.float32
    ).astype(jnp.bfloat16)
    key_grad = jnp.einsum(
        "hts,thd->shd", score_grad, query_heads, preferred_element_type=jnp.float32
    ).astype(jnp.bfloat16)
    value_grad = jnp.einsum(
        "hts,thd->shd", rounded, grad_heads, preferred_element_type=jnp.float32
    ).astype(jnp.bfloat16)
    slot_grads = jnp.concatenate(
        [
            key_grad.reshape(bin_count, block_rows, head_width),
            value_grad.reshape(bin_count, block_rows, head_width),
        ],
        axis=2,
    )
    returned = lax.all_to_all(slot_grads, "dp", split_axis=0, concat_axis=0, tiled=True)
    own_grads = jnp.dot(
        route_table,
        returned.reshape(bin_count, block_rows * 2 * head_width),
        preferred_element_type=jnp.float32,
    )
    own_grads = own_grads.astype(jnp.bfloat16).reshape(encoder_rows.shape[0], 2 * head_width)
    weight_terms = lax.dot_general(
        encoder_rows, own_grads, (((0,), (0,)), ((), ())), preferred_element_type=jnp.float32
    )
    weight_sums = lax.psum_scatter(
        weight_terms.astype(jnp.bfloat16), "dp", scatter_dimension=0, tiled=True
    ).astype(jnp.float32)
    key_weight_grad = weight_sums[:, :head_width].astype(jnp.bfloat16)
    value_weight_grad = weight_sums[:, head_width:].astype(jnp.bfloat16)
    row_terms = lax.dot_general(
        own_grads, both_weights, (((1,), (1,)), ((), ())), preferred_element_type=jnp.float32
    )
    encoder_grad = lax.psum_scatter(
        row_terms.astype(jnp.bfloat16), "mp", scatter_dimension=1, tiled=True
    )
    return (
        context.reshape(token_count, head_width),
        query_grad.reshape(token_count, head_width),
        encoder_grad,
        key_weight_grad,
        value_weight_grad,
    )


MESH = pl.DeviceIdType.MESH


def contract(a, b, dim_a, dim_b):
    return lax.dot_general(
        a, b, (((dim_a,), (dim_b,)), ((), ())), preferred_element_type=jnp.float32
    )


def step_kernel(
    n,
    count,
    q_ref,
    g_ref,
    enc_hbm,
    kw_ref,
    vw_ref,
    lengths_ref,
    bins_ref,
    docs_ref,
    held_ref,
    ctx_ref,
    qg_ref,
    eg_ref,
    kwg_ref,
    vwg_ref,
    enc,
    wts,
    wend,
    acc,
    arrived,
    tags,
    arrived_tags,
    grads,
    ret,
    own,
    gend,
    msend,
    mrecv,
    tsend,
    trecv,
    hops,
    passed,
    local_sem,
    gather_send,
    gather_recv,
    lift_send,
    lift_recv,
    core_send,
    core_recv,
    tag_send,
    tag_recv,
    out_send,
    out_recv,
    back_send,
    back_recv,
    g_send,
    g_recv,
    mid_send,
    mid_recv,
    end_send,
    end_recv,
    pair_send,
    pair_recv,
    hop_send,
    hop_recv,
):
    bf16 = jnp.bfloat16
    me, z = lax.axis_index("dp"), lax.axis_index("mp")
    core = me % 2
    x = (me // 2) % 2
    y = me // 4

    def place(py, px, pc):
        return (py * 2 + px) * 2 + pc

    at_x, at_y = place(y, 1 - x, core), place(1 - y, x, core)
    at_c, at_d = place(y, x, 1 - core), place(1 - y, 1 - x, core)
    c_x, c_y = place(y, 1 - x, 1 - core), place(1 - y, x, 1 - core)
    c_d = place(1 - y, 1 - x, 1 - core)
    depth, width = kw_ref.shape
    rows = enc.shape[0]
    blocks = rows // BLK
    blk = BLK
    heads = width // HD
    last = count - 1
    end = (z // 2) * last
    far_end = last - end
    is_end = z == end
    is_inner = z != end
    mate = z + 1 - 2 * (z % 2)
    across = last - z

    def remote(src, dst, send, recv, **device):
        return pltpu.make_async_remote_copy(
            src_ref=src,
            dst_ref=dst,
            send_sem=send,
            recv_sem=recv,
            device_id=device,
            device_id_type=MESH,
        )

    load_enc = pltpu.make_async_copy(enc_hbm, enc, local_sem.at[0])
    load_enc.start()
    barrier = pltpu.get_barrier_semaphore()
    for d in range(1, n):
        pl.semaphore_signal(
            barrier, inc=1, device_id={"dp": (me + d) % n}, device_id_type=MESH
        )
    for d in range(1, count):
        pl.semaphore_signal(
            barrier, inc=1, device_id={"mp": (z + d) % count}, device_id_type=MESH
        )

    for d in range(n):
        to = (me + d) % n
        doc = jnp.int32(-1)
        for b in range(blocks):
            doc = jnp.where(bins_ref[b] == to, docs_ref[b], doc)
        tags[to] = jnp.full(tags.shape[1:], doc.astype(jnp.float32), jnp.float32)
    pl.semaphore_wait(barrier, n - 1 + count - 1)

    def part_cols(part):
        return pl.ds(part * width, width)

    def land(src, part):
        return wts.at[src, :, part_cols(part)]

    started = []

    def ship(ident, ref, src, part, to):
        copy = remote(
            ref, land(src, part), gather_send.at[ident], gather_recv.at[ident], dp=to
        )
        copy.start()
        started.append(copy)

    def landed(ident, src, part):
        remote(
            land(src, part), land(src, part), gather_send.at[ident], gather_recv.at[ident], dp=at_c
        ).wait_recv()

    def lifted(src, part):
        slot = (src // 2 - 1 + end // last) * 2 + src % 2
        return wend.at[slot, :, part_cols(part)]

    ours, theirs = (me, at_x, at_y, at_d), (at_c, c_x, c_y, c_d)
    pieces = [(0, 0), (0, 1), (1, 0), (2, 1), (1, 1), (2, 0), (3, 0), (3, 1)]

    def lift(i, part, ref=None):
        src = ours[i]
        ident = 2 * i + part

        @pl.when(jnp.logical_and(is_end, src // 2 != end))
        def _():
            remote(
                land(src, part) if ref is None else ref,
                lifted(src, part),
                lift_send.at[ident],
                lift_recv.at[ident],
                mp=mate,
            ).start()

    def each_piece(todo, listed, of_end):
        for i, part in listed:
            for src, mirror in ((ours[i], theirs[i]),):

                @pl.when(jnp.logical_and(is_end if of_end else is_inner, src // 2 != end))
                def _():
                    todo(i, part, src, mirror)

    def lift_copy(i, part, src):
        ident = 2 * i + part
        return remote(
            lifted(src, part), lifted(src, part), lift_send.at[ident], lift_recv.at[ident], mp=mate
        )

    def core_copy(i, part, src):
        ident = 2 * i + part
        return remote(
            lifted(src, part), lifted(src, part), core_send.at[ident], core_recv.at[ident], dp=at_c
        )

    def hand_over(i, part, src, mirror):
        lift_copy(i, part, src).wait_recv()
        core_copy(i, part, src).start()

    ship(0, kw_ref, me, 0, at_x)
    ship(3, vw_ref, me, 1, at_y)
    ship(1, vw_ref, me, 1, at_x)
    ship(2, kw_ref, me, 0, at_y)
    ship(6, kw_ref, me, 0, at_c)
    ship(7, vw_ref, me, 1, at_c)
    lift(0, 0, kw_ref)
    lift(0, 1, vw_ref)
    own_k = pltpu.make_async_copy(kw_ref, land(me, 0), local_sem.at[1])
    own_v = pltpu.make_async_copy(vw_ref, land(me, 1), local_sem.at[2])
    own_k.start()
    own_v.start()
    tag_copies = []
    for d in range(1, n):
        to = (me + d) % n
        copy = remote(
            tags.at[to], arrived_tags.at[me], tag_send.at[d], tag_recv.at[d], dp=to
        )
        copy.start()
        tag_copies.append(copy)
    arrived_tags[me] = tags[me]
    own_k.wait()
    own_v.wait()
    load_enc.wait()

    def multiply(src, part, first=False):
        columns = pl.ds(pl.multiple_of(src * depth, depth), depth)

        @pl.loop(0, width // HD)
        def _(t):
            cols = pl.ds(pl.multiple_of(part * width + t * HD, HD), HD)
            product = jnp.dot(
                enc[:, columns], wts[src, :, cols], preferred_element_type=jnp.float32
            ).reshape(blocks, blk, HD)
            if first:
                acc[:, :, cols] = product
            else:
                acc[:, :, cols] += product

    multiply(me, 0, True)
    multiply(me, 1, True)
    landed(6, at_c, 0)
    multiply(at_c, 0)
    landed(7, at_c, 1)
    multiply(at_c, 1)
    landed(0, at_x, 0)
    ship(4, land(at_x, 0), at_x, 0, at_y)
    ship(8, land(at_x, 0), at_x, 0, at_c)
    lift(1, 0)
    landed(3, at_y, 1)
    ship(5, land(at_y, 1), at_y, 1, at_x)
    ship(11, land(at_y, 1), at_y, 1, at_c)
    lift(2, 1)
    multiply(at_x, 0)
    multiply(at_y, 1)
    landed(8, c_x, 0)
    multiply(c_x, 0)
    landed(11, c_y, 1)
    multiply(c_y, 1)
    landed(1, at_x, 1)
    ship(9, land(at_x, 1), at_x, 1, at_c)
    lift(1, 1)
    landed(2, at_y, 0)
    ship(10, land(at_y, 0), at_y, 0, at_c)
    lift(2, 0)
    multiply(at_x, 1)
    multiply(at_y, 0)
    landed(9, c_x, 1)
    multiply(c_x, 1)
    landed(10, c_y, 0)
    multiply(c_y, 0)
    landed(4, at_d, 0)
    ship(12, land(at_d, 0), at_d, 0, at_c)
    lift(3, 0)
    landed(5, at_d, 1)
    ship(13, land(at_d, 1), at_d, 1, at_c)
    lift(3, 1)
    multiply(at_d, 0)
    multiply(at_d, 1)
    landed(12, c_d, 0)
    multiply(c_d, 0)
    landed(13, c_d, 1)
    multiply(c_d, 1)

    out_copies = []
    mine = pl.ds(pl.multiple_of(me * blk, blk), blk)
    for d in [*range(1, n), 0]:
        to = (me + d) % n
        msend[d // blocks, d % blocks] = acc[held_ref[to]].astype(bf16)

        if d == 0:
            arrived[mine, :] = msend[0, 0]
            continue
        copy = remote(
            msend.at[d // blocks, d % blocks], arrived.at[mine, :], out_send.at[d], out_recv.at[d], dp=to
        )
        copy.start()
        out_copies.append(copy)

    each_piece(hand_over, pieces[:4], False)
    position = lax.broadcasted_iota(jnp.int32, (q_ref.shape[0], 1), 0)
    token_doc = jnp.zeros(position.shape, jnp.float32)
    doc_end = jnp.int32(0)
    for k in range(lengths_ref.shape[1]):
        doc_end = doc_end + lengths_ref[0, k]
        token_doc = token_doc + jnp.where(position >= doc_end, 1.0, 0.0)
    for copy in tag_copies:
        copy.wait()
    for copy in out_copies:
        copy.wait()
    tag_row = jnp.concatenate([arrived_tags[s, 0:1, :] for s in range(n)], axis=1)
    live = tag_row == token_doc
    present = jnp.max(jnp.where(live, 1.0, 0.0), axis=1, keepdims=True) > 0.0
    scaling = HD ** (-0.5)
    back_copies = []
    for h in range(heads):
        hk, hv = pl.ds(h * HD, HD), pl.ds(width + h * HD, HD)
        q, g = q_ref[:, hk], g_ref[:, hk]
        scores = contract(q, arrived[:, hk], 1, 1) * scaling
        highest = jnp.max(jnp.where(live, scores, masked_value), axis=1, keepdims=True)
        highest = jnp.where(present, highest, 0.0)
        raised = jnp.exp(jnp.where(live, scores - highest, masked_value))
        totals = jnp.maximum(jnp.sum(raised, axis=1, keepdims=True), 1.0)
        attention = raised / totals
        rounded = attention.astype(bf16)
        grad_raw = contract(g, arrived[:, hv], 1, 1)
        deltas = jnp.sum(attention * grad_raw, axis=1, keepdims=True)
        score_grad = (attention * (grad_raw - deltas) * scaling).astype(bf16)
        grads[:, h, 0] = contract(score_grad, q, 0, 0).astype(bf16).reshape(n, blk, HD)
        grads[:, h, 1] = contract(rounded, g, 0, 0).astype(bf16).reshape(n, blk, HD)
        for d in range(1, n):
            to = (me + d) % n
            copy = remote(
                grads.at[to, h],
                ret.at[me, h],
                back_send.at[h, d],
                back_recv.at[h, d],
                dp=to,
            )
            copy.start()
            back_copies.append(copy)
        ret[me, h] = grads[me, h]
        ctx_ref[:, hk] = jnp.dot(
            rounded, arrived[:, hv], preferred_element_type=jnp.float32
        ).astype(bf16)
        qg_ref[:, hk] = jnp.dot(
            score_grad, arrived[:, hk], preferred_element_type=jnp.float32
        ).astype(bf16)
    each_piece(hand_over, pieces[4:], False)
    for copy in back_copies:
        copy.wait()

    def block(r):
        return pl.ds(r * blk if isinstance(r, int) else pl.multiple_of(r * blk, blk), blk)

    def g_copy(r):
        return remote(own.at[block(r), :], gend.at[r], g_send.at[r], g_recv.at[r], mp=mate)

    def mid_copy(way, r):
        return remote(
            msend.at[way, r], mrecv.at[way, r], mid_send.at[way, r], mid_recv.at[way, r], mp=across
        )

    def end_copy(r):
        return remote(arrived.at[block(r), :], gend.at[r], end_send.at[r], end_recv.at[r], mp=mate)

    def pair_copy(i):
        return remote(tsend.at[i], trecv.at[i], pair_send.at[i], pair_recv.at[i], dp=at_c)

    def hop_copy(way, i, src):
        to = at_x if (way == 0) == (i < 2) else at_y
        return remote(src, hops.at[way, i], hop_send.at[way, i], hop_recv.at[way, i], dp=to)

    for r in range(blocks):
        for h in range(heads):
            own[block(r), pl.ds(h * HD, HD)] = ret[bins_ref[r], h, 0]
            own[block(r), pl.ds(width + h * HD, HD)] = ret[bins_ref[r], h, 1]

        @pl.when(is_end)
        def _():
            g_copy(r).start()

    for i, part in pieces:
        mirror = theirs[i]

        @pl.when(jnp.logical_and(is_inner, mirror // 2 != end))
        def _():
            core_copy(i, part, mirror).wait_recv()

    def own_weights(d, j):
        return wts[2 * d + j]

    def end_weights(d, j):
        return wend[(d - 1 + end // last) * 2 + j]

    def shard_of(i, parity):
        flip_x, flip_y = 1 - i // 2, 1 - i % 2
        px = x + flip_x - 2 * x * flip_x
        py = y + flip_y - 2 * y * flip_y
        return place(py, px, parity)

    def term(shard, cols):
        columns = pl.ds(pl.multiple_of(shard * depth, depth), depth)
        return contract(enc[:, columns], own[:, cols], 0, 0).astype(bf16)

    def half_cols(j):
        return pl.ds(pl.multiple_of(j * width, width), width)

    @pl.loop(0, blocks)
    def _(r):
        @pl.when(r < 2)
        def _():
            @pl.loop(0, 2)
            def _(k):
                i = 2 * r + k
                shard = shard_of(i, 1 - core)

                @pl.loop(0, 2)
                def _(j):
                    tsend[i, :, half_cols(j)] = term(shard, half_cols(j))

                pair_copy(i).start()

        @pl.when(is_inner)
        def _():
            g_copy(r).wait_recv()
            for way, dest in ((0, far_end), (1, across)):

                @pl.loop(0, 2)
                def _(j):
                    summed = contract(own[block(r), :], own_weights(dest, j), 1, 1)
                    summed += contract(gend[r], end_weights(dest, j), 1, 1)
                    msend[way, r, :, half_cols(j)] = summed.astype(bf16)

                mid_copy(way, r).start()

        @pl.when(jnp.logical_and(r >= 2, r < 4))
        def _():
            @pl.loop(0, 2)
            def _(k):
                i = 2 * (r - 2) + k
                shard = shard_of(i, core)
                pair_copy(i).wait_recv()

                @pl.loop(0, 2)
                def _(j):
                    cols = half_cols(j)
                    summed = term(shard, cols).astype(jnp.float32)
                    summed += trecv[i, :, cols].astype(jnp.float32)
                    trecv[i, :, cols] = summed.astype(bf16)

        @pl.when(r == 2)
        def _():
            hop_copy(0, 1, trecv.at[0, :, part_cols(0)]).start()
            hop_copy(0, 0, trecv.at[1, :, part_cols(0)]).start()
            hop_copy(1, 1, trecv.at[0, :, part_cols(1)]).start()

        @pl.when(r == 3)
        def _():
            hop_copy(1, 0, trecv.at[2, :, part_cols(1)]).start()

    for way in range(2):
        hop_copy(way, 1, hops.at[way, 1]).wait_recv()
        summed = trecv[2 - way, :, part_cols(way)].astype(jnp.float32)
        summed += hops[way, 1].astype(jnp.float32)
        passed[way] = summed.astype(bf16)
        hop_copy(way, 2, passed.at[way]).start()

    total = acc.at[0]

    @pl.loop(0, blocks)
    def _(r):
        @pl.when(is_inner)
        def _():
            @pl.loop(0, 2)
            def _(j):
                total[:, half_cols(j)] = contract(own[block(r), :], own_weights(end, j), 1, 1)

            mid_copy(0, r).wait_recv()
            arrived[block(r), :] = (total[...] + mrecv[0, r].astype(jnp.float32)).astype(bf16)
            end_copy(r).start()

            @pl.loop(0, 2)
            def _(j):
                summed = contract(own[block(r), :], own_weights(z, j), 1, 1)
                summed += contract(gend[r], end_weights(z, j), 1, 1)
                total[:, half_cols(j)] = summed

            mid_copy(1, r).wait_recv()
            eg_ref[block(r), :] = (total[...] + mrecv[1, r].astype(jnp.float32)).astype(bf16)

        @pl.when(is_end)
        def _():
            @pl.loop(0, 2)
            def _(j):
                total[:, half_cols(j)] = contract(own[block(r), :], own_weights(z, j), 1, 1)

            end_copy(r).wait_recv()
            eg_ref[block(r), :] = (total[...] + gend[r].astype(jnp.float32)).astype(bf16)

        @pl.when(r == blocks - 2)
        def _():
            for way, out in ((0, kwg_ref), (1, vwg_ref)):
                hop_copy(way, 0, hops.at[way, 0]).wait_recv()
                hop_copy(way, 2, hops.at[way, 2]).wait_recv()
                summed = trecv[3, :, part_cols(way)].astype(jnp.float32)
                summed += hops[way, 0].astype(jnp.float32) + hops[way, 2].astype(jnp.float32)
                out[...] = summed.astype(bf16)

    for copy in started:
        copy.wait_send()
    each_piece(lambda i, part, src, mirror: lift_copy(i, part, src).wait_send(), pieces, True)
    each_piece(lambda i, part, src, mirror: core_copy(i, part, src).wait_send(), pieces, False)

    @pl.loop(0, blocks)
    def _(r):
        @pl.when(is_end)
        def _():
            g_copy(r).wait_send()

        @pl.when(is_inner)
        def _():
            mid_copy(0, r).wait_send()
            mid_copy(1, r).wait_send()
            end_copy(r).wait_send()

    for i in range(4):
        pair_copy(i).wait_send()
    for way in range(2):
        for i in range(3):
            hop_copy(way, i, hops.at[way, i]).wait_send()


def per_device_cube(
    queries,
    context_grad,
    encoder_rows,
    key_weight,
    value_weight,
    document_lengths,
    block_bin,
    block_document,
):
    n, count = lax.axis_size("dp"), lax.axis_size("mp")
    rows, model = encoder_rows.shape
    depth, width = key_weight.shape
    heads = width // HD
    tokens = queries.shape[0]
    blocks = rows // BLK
    chips = n // 2
    hits = block_bin[:, None] == jnp.arange(n, dtype=jnp.int32)[None, :]
    held = jnp.sum(jnp.where(hits, jnp.arange(blocks, dtype=jnp.int32)[:, None], 0), axis=0)
    vmem = pl.BlockSpec(memory_space=pltpu.VMEM)
    smem = pl.BlockSpec(memory_space=pltpu.SMEM)
    hbm = pl.BlockSpec(memory_space=pl.ANY)
    bf16 = jnp.bfloat16
    dma = pltpu.SemaphoreType.DMA
    shape = jax.ShapeDtypeStruct
    pairs = []
    for extent in [(14,), (8,), (8,), (n,), (n,), (heads, n), (blocks,), (2, blocks), (blocks,), (chips,), (2, 3)]:
        pairs += [dma(extent), dma(extent)]
    return pl.pallas_call(
        functools.partial(step_kernel, n, count),
        out_shape=(
            shape((tokens, width), bf16),
            shape((tokens, width), bf16),
            shape((rows, model // count), bf16),
            shape((depth, width), bf16),
            shape((depth, width), bf16),
        ),
        in_specs=[vmem, vmem, hbm, vmem, vmem, smem, smem, smem, smem],
        out_specs=(vmem,) * 5,
        scratch_shapes=[
            pltpu.VMEM((rows, model), bf16),
            pltpu.VMEM((n, depth, 2 * width), bf16),
            pltpu.VMEM((n - 2, depth, 2 * width), bf16),
            pltpu.VMEM((blocks, BLK, 2 * width), jnp.float32),
            pltpu.VMEM((n * BLK, 2 * width), bf16),
            pltpu.VMEM((n, 8, BLK), jnp.float32),
            pltpu.VMEM((n, 8, BLK), jnp.float32),
            pltpu.VMEM((n, heads, 2, BLK, HD), bf16),
            pltpu.VMEM((n, heads, 2, BLK, HD), bf16),
            pltpu.VMEM((rows, 2 * width), bf16),
            pltpu.VMEM((blocks, BLK, 2 * width), bf16),
            pltpu.VMEM((2, blocks, BLK, 2 * width), bf16),
            pltpu.VMEM((2, blocks, BLK, 2 * width), bf16),
            pltpu.VMEM((chips, depth, 2 * width), bf16),
            pltpu.VMEM((chips, depth, 2 * width), bf16),
            pltpu.VMEM((2, 3, depth, width), bf16),
            pltpu.VMEM((2, depth, width), bf16),
            dma((3,)),
            *pairs,
        ],
        compiler_params=pltpu.CompilerParams(
            collective_id=0, has_side_effects=True, vmem_limit_bytes=67043328
        ),
    )(
        queries,
        context_grad,
        encoder_rows,
        key_weight,
        value_weight,
        document_lengths,
        block_bin,
        block_document,
        held,
    )


def solution(mesh):
    in_specs = (
        P("dp", "mp"),
        P("dp", "mp"),
        P("dp", None),
        P("dp", "mp"),
        P("dp", "mp"),
        P("dp", None),
        P("dp"),
        P("dp"),
    )
    out_specs = (P("dp", "mp"), P("dp", "mp"), P("dp", "mp"), P("dp", "mp"), P("dp", "mp"))
    cube = mesh.shape["dp"] == 2 * 2 * 2 and mesh.shape["mp"] == 2 * 2
    return jax.shard_map(
        per_device_cube if cube else per_device, mesh=mesh, in_specs=in_specs, out_specs=out_specs, check_vma=False
    )
```

time: 299 us -> 199 us (0.67)
  the two profiles are of different devices: /device:TPU:10 before, /device:TPU:0 now
where the time goes in v1:
time: 199 us; the launch traced here: 195 us
  Pallas kernels  186 us (93%)
  local copies, waits for them, and re-layouts  7.89 us (4%)
    pallas_call x1, Pallas kernels, per_device_cube(): pl.pallas_call(functools.partial(step_kernel, n, count), out_shape=(shape...  186 us
    unnamed x9, local copies, waits for them, and re-layouts  7.89 us

profile of v1, /device:TPU:0, one launch (start us, length us, event | category | flops | bytes accessed | tf_op | source)
XLA Modules:
  0.0 195.5 jit_solution(11857023775537371994)
XLA Ops:
  0.6 1.2 select_reduce_fusion.held_ref
  1.9 185.7 %shard_map.119 = (bf16[256,512]{1,0:T(8,128)(2,1)}, bf16[256,512]{1,0:T(8,128)(2,1)}, bf16[896,1024]{1,0:T(8,128)(2,1)}, bf16[512,512]{1,0:T(8,128)(2,1)}, bf16[512,512]{1,0:T(8,128)(2,1)}) custom-call(bf16[256,512]{1,0:T(8,128)(2,1)} %q_ref.1, bf16[256,512]{1,0:T(8,128)(2,1)} %g_ref.1, bf16[896,4096]{1,0:T(8,128)(2,1)} %enc_hbm.1, bf16[512,512]{1,0:T(8,128)(2,1)} %kw_ref.1, ...), custom_call_target="tpu_custom_call" | custom-call | tf_op jit(solution)/shard_map/pallas_call | solution.py:694
  187.6 1.7 copy.18
  189.2 1.7 copy.19
  190.9 0.0 copy-start.1
  190.9 0.0 copy-start
  190.9 3.0 %copy.20 = bf16[896,1024]{1,0:T(8,128)(2,1)} copy(bf16[896,1024]{1,0:T(8,128)(2,1)} %get-tuple-element.12) | data formatting | bytes 3670016
  193.9 0.0 copy-done.1
  193.9 0.8 copy.21
  194.7 0.0 copy-done
  194.7 0.8 copy.22
Async XLA Ops:
  190.9 3.0 %copy-start.1 = (bf16[512,512]{1,0:T(8,128)(2,1)S(1)}, bf16[512,512]{1,0:T(8,128)(2,1)}, u32[]{:S(2)}) copy-start(bf16[512,512]{1,0:T(8,128)(2,1)} %get-tuple-element.13) | copy-start | bytes 1572868
  190.9 3.8 %copy-start = (bf16[512,512]{1,0:T(8,128)(2,1)S(1)}, bf16[512,512]{1,0:T(8,128)(2,1)}, u32[]{:S(2)}) copy-start(bf16[512,512]{1,0:T(8,128)(2,1)} %get-tuple-element.14) | copy-start | bytes 1572868

commit v2 on v1

--- a/solution.py
+++ b/solution.py
@@ -162,7 +162,7 @@
     lengths_ref,
     bins_ref,
     docs_ref,
-    held_ref,
+    table_ref,
     ctx_ref,
     qg_ref,
     eg_ref,
@@ -179,6 +179,7 @@
     ret,
     own,
     gend,
+    pend,
     msend,
     mrecv,
     tsend,
@@ -204,6 +205,8 @@
     mid_recv,
     end_send,
     end_recv,
+    prod_send,
+    prod_recv,
     pair_send,
     pair_recv,
     hop_send,
@@ -227,9 +230,11 @@
     blocks = rows // BLK
     blk = BLK
     heads = width // HD
+    tokens = q_ref.shape[0]
     last = count - 1
     end = (z // 2) * last
     far_end = last - end
+    side = z // 2
     is_end = z == end
     is_inner = z != end
     mate = z + 1 - 2 * (z % 2)
@@ -286,8 +291,7 @@
         ).wait_recv()
 
     def lifted(src, part):
-        slot = (src // 2 - 1 + end // last) * 2 + src % 2
-        return wend.at[slot, :, part_cols(part)]
+        return wend.at[src % 4, :, part_cols(part)]
 
     ours, theirs = (me, at_x, at_y, at_d), (at_c, c_x, c_y, c_d)
     pieces = [(0, 0), (0, 1), (1, 0), (2, 1), (1, 1), (2, 0), (3, 0), (3, 1)]
@@ -296,7 +300,7 @@
         src = ours[i]
         ident = 2 * i + part
 
-        @pl.when(jnp.logical_and(is_end, src // 2 != end))
+        @pl.when(jnp.logical_and(is_end, src // 4 != side))
         def _():
             remote(
                 land(src, part) if ref is None else ref,
@@ -308,11 +312,10 @@
 
     def each_piece(todo, listed, of_end):
         for i, part in listed:
-            for src, mirror in ((ours[i], theirs[i]),):
-
-                @pl.when(jnp.logical_and(is_end if of_end else is_inner, src // 2 != end))
-                def _():
-                    todo(i, part, src, mirror)
+
+            @pl.when(jnp.logical_and(is_end if of_end else is_inner, ours[i] // 4 != side))
+            def _():
+                todo(i, part, ours[i], theirs[i])
 
     def lift_copy(i, part, src):
         ident = 2 * i + part
@@ -414,23 +417,42 @@
     landed(13, c_d, 1)
     multiply(c_d, 1)
 
-    out_copies = []
-    mine = pl.ds(pl.multiple_of(me * blk, blk), blk)
-    for d in [*range(1, n), 0]:
-        to = (me + d) % n
-        msend[d // blocks, d % blocks] = acc[held_ref[to]].astype(bf16)
-
-        if d == 0:
-            arrived[mine, :] = msend[0, 0]
-            continue
-        copy = remote(
-            msend.at[d // blocks, d % blocks], arrived.at[mine, :], out_send.at[d], out_recv.at[d], dp=to
-        )
-        copy.start()
-        out_copies.append(copy)
-
-    each_piece(hand_over, pieces[:4], False)
-    position = lax.broadcasted_iota(jnp.int32, (q_ref.shape[0], 1), 0)
+    def rows_of(slot):
+        return pl.ds(pl.multiple_of(slot * blk, blk), blk)
+
+    def slot_at(i):
+        flip_c, flip_x, flip_y = i % 2, (i // 2) % 2, i // 4
+        return place(
+            y + flip_y - 2 * y * flip_y,
+            x + flip_x - 2 * x * flip_x,
+            core + flip_c - 2 * core * flip_c,
+        )
+
+    def out_copy(h, i):
+        to = slot_at(i)
+        return remote(
+            grads.at[h, :, rows_of(to), :],
+            arrived.at[h, :, rows_of(me), :],
+            out_send.at[h, i],
+            out_recv.at[h, i],
+            dp=to,
+        )
+
+    for h in range(heads):
+        for i in [*range(1, n), 0]:
+            to = slot_at(i)
+            for part in range(2):
+                cols = pl.ds(part * width + h * HD, HD)
+                picked = acc[table_ref[0, to], :, cols].astype(bf16)
+                if i == 0:
+                    arrived[h, part, rows_of(me), :] = picked
+                else:
+                    grads[h, part, rows_of(to), :] = picked
+            if i > 0:
+                out_copy(h, i).start()
+
+    each_piece(hand_over, pieces[:6], False)
+    position = lax.broadcasted_iota(jnp.int32, (tokens, 1), 0)
     token_doc = jnp.zeros(position.shape, jnp.float32)
     doc_end = jnp.int32(0)
     for k in range(lengths_ref.shape[1]):
@@ -438,55 +460,56 @@
         token_doc = token_doc + jnp.where(position >= doc_end, 1.0, 0.0)
     for copy in tag_copies:
         copy.wait()
-    for copy in out_copies:
-        copy.wait()
     tag_row = jnp.concatenate([arrived_tags[s, 0:1, :] for s in range(n)], axis=1)
     live = tag_row == token_doc
     present = jnp.max(jnp.where(live, 1.0, 0.0), axis=1, keepdims=True) > 0.0
     scaling = HD ** (-0.5)
-    back_copies = []
     for h in range(heads):
-        hk, hv = pl.ds(h * HD, HD), pl.ds(width + h * HD, HD)
+        for i in range(1, n):
+            out_copy(h, i).wait()
+        hk = pl.ds(h * HD, HD)
         q, g = q_ref[:, hk], g_ref[:, hk]
-        scores = contract(q, arrived[:, hk], 1, 1) * scaling
+        scores = contract(q, arrived[h, 0], 1, 1) * scaling
         highest = jnp.max(jnp.where(live, scores, masked_value), axis=1, keepdims=True)
         highest = jnp.where(present, highest, 0.0)
         raised = jnp.exp(jnp.where(live, scores - highest, masked_value))
         totals = jnp.maximum(jnp.sum(raised, axis=1, keepdims=True), 1.0)
         attention = raised / totals
         rounded = attention.astype(bf16)
-        grad_raw = contract(g, arrived[:, hv], 1, 1)
+        grad_raw = contract(g, arrived[h, 1], 1, 1)
         deltas = jnp.sum(attention * grad_raw, axis=1, keepdims=True)
         score_grad = (attention * (grad_raw - deltas) * scaling).astype(bf16)
-        grads[:, h, 0] = contract(score_grad, q, 0, 0).astype(bf16).reshape(n, blk, HD)
-        grads[:, h, 1] = contract(rounded, g, 0, 0).astype(bf16).reshape(n, blk, HD)
-        for d in range(1, n):
-            to = (me + d) % n
-            copy = remote(
-                grads.at[to, h],
-                ret.at[me, h],
-                back_send.at[h, d],
-                back_recv.at[h, d],
-                dp=to,
-            )
-            copy.start()
-            back_copies.append(copy)
-        ret[me, h] = grads[me, h]
+        grads[h, 0] = contract(score_grad, q, 0, 0).astype(bf16)
+        grads[h, 1] = contract(rounded, g, 0, 0).astype(bf16)
+        tsend[h, pl.ds(0, tokens), :] = rounded
+        tsend[h, pl.ds(tokens, tokens), :] = score_grad
+        if h == 0:
+            each_piece(hand_over, pieces[6:], False)
+
+    def back_copy(i):
+        to = slot_at(i)
+        return remote(
+            grads.at[:, :, rows_of(to), :],
+            ret.at[:, :, rows_of(me), :],
+            back_send.at[i],
+            back_recv.at[i],
+            dp=to,
+        )
+
+    for i in range(1, n):
+        back_copy(i).start()
+    ret[:, :, rows_of(me), :] = grads[:, :, rows_of(me), :]
+    for h in range(heads):
+        hk = pl.ds(h * HD, HD)
         ctx_ref[:, hk] = jnp.dot(
-            rounded, arrived[:, hv], preferred_element_type=jnp.float32
+            tsend[h, pl.ds(0, tokens), :], arrived[h, 1], preferred_element_type=jnp.float32
         ).astype(bf16)
         qg_ref[:, hk] = jnp.dot(
-            score_grad, arrived[:, hk], preferred_element_type=jnp.float32
+            tsend[h, pl.ds(tokens, tokens), :], arrived[h, 0], preferred_element_type=jnp.float32
         ).astype(bf16)
-    each_piece(hand_over, pieces[4:], False)
-    for copy in back_copies:
-        copy.wait()
-
-    def block(r):
-        return pl.ds(r * blk if isinstance(r, int) else pl.multiple_of(r * blk, blk), blk)
 
     def g_copy(r):
-        return remote(own.at[block(r), :], gend.at[r], g_send.at[r], g_recv.at[r], mp=mate)
+        return remote(own.at[r], gend.at[r], g_send.at[r], g_recv.at[r], mp=mate)
 
     def mid_copy(way, r):
         return remote(
@@ -494,7 +517,10 @@
         )
 
     def end_copy(r):
-        return remote(arrived.at[block(r), :], gend.at[r], end_send.at[r], end_recv.at[r], mp=mate)
+        return remote(mrecv.at[0, r], mrecv.at[0, r], end_send.at[r], end_recv.at[r], mp=mate)
+
+    def prod_copy(r):
+        return remote(msend.at[0, r], pend.at[r], prod_send.at[r], prod_recv.at[r], mp=mate)
 
     def pair_copy(i):
         return remote(tsend.at[i], trecv.at[i], pair_send.at[i], pair_recv.at[i], dp=at_c)
@@ -503,27 +529,39 @@
         to = at_x if (way == 0) == (i < 2) else at_y
         return remote(src, hops.at[way, i], hop_send.at[way, i], hop_recv.at[way, i], dp=to)
 
-    for r in range(blocks):
+    for i, part in pieces:
+
+        @pl.when(jnp.logical_and(is_inner, theirs[i] // 4 != side))
+        def _():
+            core_copy(i, part, theirs[i]).wait_recv()
+
+    def collect(r):
+        back_copy_at = slot_at(r + 1)
+        remote(
+            ret.at[:, :, rows_of(back_copy_at), :],
+            ret.at[:, :, rows_of(back_copy_at), :],
+            back_send.at[r + 1],
+            back_recv.at[r + 1],
+            dp=at_c,
+        ).wait_recv()
+        later = table_ref[2, r] > 0
         for h in range(heads):
-            own[block(r), pl.ds(h * HD, HD)] = ret[bins_ref[r], h, 0]
-            own[block(r), pl.ds(width + h * HD, HD)] = ret[bins_ref[r], h, 1]
+            for part in range(2):
+                own[r, :, pl.ds(part * width + h * HD, HD)] = jnp.where(
+                    later,
+                    ret[h, part, rows_of(back_copy_at), :],
+                    ret[h, part, rows_of(slot_at(r)), :],
+                )
 
         @pl.when(is_end)
         def _():
             g_copy(r).start()
-
-    for i, part in pieces:
-        mirror = theirs[i]
-
-        @pl.when(jnp.logical_and(is_inner, mirror // 2 != end))
-        def _():
-            core_copy(i, part, mirror).wait_recv()
 
     def own_weights(d, j):
         return wts[2 * d + j]
 
     def end_weights(d, j):
-        return wend[(d - 1 + end // last) * 2 + j]
+        return wend[(d % 2) * 2 + j]
 
     def shard_of(i, parity):
         flip_x, flip_y = 1 - i // 2, 1 - i % 2
@@ -531,65 +569,93 @@
         py = y + flip_y - 2 * y * flip_y
         return place(py, px, parity)
 
-    def term(shard, cols):
+    def term(shard, part, h):
         columns = pl.ds(pl.multiple_of(shard * depth, depth), depth)
-        return contract(enc[:, columns], own[:, cols], 0, 0).astype(bf16)
+        return contract(enc[:, columns], ret[h, part, pl.ds(0, rows), :], 0, 0).astype(bf16)
+
+    def each_slab(todo):
+        for part in range(2):
+            for h in range(heads):
+                todo(part, h, pl.ds(part * width + h * HD, HD))
 
     def half_cols(j):
         return pl.ds(pl.multiple_of(j * width, width), width)
 
     @pl.loop(0, blocks)
     def _(r):
-        @pl.when(r < 2)
-        def _():
-            @pl.loop(0, 2)
-            def _(k):
-                i = 2 * r + k
-                shard = shard_of(i, 1 - core)
+        @pl.when(r < 3)
+        def _():
+            collect(r)
+
+        @pl.when(is_inner)
+        def _():
+            g_copy(r).wait_recv()
+            for way, dest in ((0, far_end), (1, across)):
 
                 @pl.loop(0, 2)
                 def _(j):
-                    tsend[i, :, half_cols(j)] = term(shard, half_cols(j))
-
-                pair_copy(i).start()
-
-        @pl.when(is_inner)
-        def _():
-            g_copy(r).wait_recv()
-            for way, dest in ((0, far_end), (1, across)):
-
-                @pl.loop(0, 2)
-                def _(j):
-                    summed = contract(own[block(r), :], own_weights(dest, j), 1, 1)
+                    summed = contract(own[r], own_weights(dest, j), 1, 1)
                     summed += contract(gend[r], end_weights(dest, j), 1, 1)
                     msend[way, r, :, half_cols(j)] = summed.astype(bf16)
 
                 mid_copy(way, r).start()
 
-        @pl.when(jnp.logical_and(r >= 2, r < 4))
-        def _():
-            @pl.loop(0, 2)
-            def _(k):
-                i = 2 * (r - 2) + k
+        @pl.when(r == 2)
+        def _():
+            @pl.loop(3, blocks)
+            def _(later):
+                collect(later)
+
+            for b in range(blocks):
+                block = own[table_ref[1, b]]
+                for h in range(heads):
+                    for part in range(2):
+                        first = part * width + h * HD
+                        ret[h, part, pl.ds(b * blk, blk), :] = block[:, first : first + HD]
+
+            @pl.loop(0, 4)
+            def _(i):
+                shard = shard_of(i, 1 - core)
+
+                def fill(part, h, cols):
+                    tsend[i, :, cols] = term(shard, part, h)
+
+                each_slab(fill)
+                pair_copy(i).start()
+
+        @pl.when(r == 3)
+        def _():
+            @pl.loop(0, 4)
+            def _(i):
                 shard = shard_of(i, core)
                 pair_copy(i).wait_recv()
 
-                @pl.loop(0, 2)
-                def _(j):
-                    cols = half_cols(j)
-                    summed = term(shard, cols).astype(jnp.float32)
+                def fill(part, h, cols):
+                    summed = term(shard, part, h).astype(jnp.float32)
                     summed += trecv[i, :, cols].astype(jnp.float32)
                     trecv[i, :, cols] = summed.astype(bf16)
 
-        @pl.when(r == 2)
-        def _():
-            hop_copy(0, 1, trecv.at[0, :, part_cols(0)]).start()
-            hop_copy(0, 0, trecv.at[1, :, part_cols(0)]).start()
-            hop_copy(1, 1, trecv.at[0, :, part_cols(1)]).start()
-
-        @pl.when(r == 3)
-        def _():
-            hop_copy(1, 0, trecv.at[2, :, part_cols(1)]).start()
+                each_slab(fill)
+
+                @pl.when(i == 1)
+                def _():
+                    hop_copy(0, 1, trecv.at[0, :, part_cols(0)]).start()
+                    hop_copy(0, 0, trecv.at[1, :, part_cols(0)]).start()
+                    hop_copy(1, 1, trecv.at[0, :, part_cols(1)]).start()
+
+                @pl.when(i == 2)
+                def _():
+                    hop_copy(1, 0, trecv.at[2, :, part_cols(1)]).start()
+
+    @pl.when(is_end)
+    def _():
+        @pl.loop(0, blocks)
+        def _(r):
+            @pl.loop(0, 2)
+            def _(j):
+                msend[0, r, :, half_cols(j)] = contract(own[r], own_weights(mate, j), 1, 1).astype(bf16)
+
+            prod_copy(r).start()
 
     for way in range(2):
         hop_copy(way, 1, hops.at[way, 1]).wait_recv()
@@ -600,35 +666,30 @@
 
     total = acc.at[0]
 
+    def own_product(r, dest):
+        @pl.loop(0, 2)
+        def _(j):
+            total[:, half_cols(j)] = contract(own[r], own_weights(dest, j), 1, 1)
+
     @pl.loop(0, blocks)
     def _(r):
         @pl.when(is_inner)
         def _():
-            @pl.loop(0, 2)
-            def _(j):
-                total[:, half_cols(j)] = contract(own[block(r), :], own_weights(end, j), 1, 1)
-
+            own_product(r, end)
             mid_copy(0, r).wait_recv()
-            arrived[block(r), :] = (total[...] + mrecv[0, r].astype(jnp.float32)).astype(bf16)
+            mrecv[0, r] = (total[...] + mrecv[0, r].astype(jnp.float32)).astype(bf16)
             end_copy(r).start()
-
-            @pl.loop(0, 2)
-            def _(j):
-                summed = contract(own[block(r), :], own_weights(z, j), 1, 1)
-                summed += contract(gend[r], end_weights(z, j), 1, 1)
-                total[:, half_cols(j)] = summed
-
+            own_product(r, z)
+            prod_copy(r).wait_recv()
+            total[...] += pend[r].astype(jnp.float32)
             mid_copy(1, r).wait_recv()
-            eg_ref[block(r), :] = (total[...] + mrecv[1, r].astype(jnp.float32)).astype(bf16)
+            eg_ref[r] = (total[...] + mrecv[1, r].astype(jnp.float32)).astype(bf16)
 
         @pl.when(is_end)
         def _():
-            @pl.loop(0, 2)
-            def _(j):
-                total[:, half_cols(j)] = contract(own[block(r), :], own_weights(z, j), 1, 1)
-
+            own_product(r, z)
             end_copy(r).wait_recv()
-            eg_ref[block(r), :] = (total[...] + gend[r].astype(jnp.float32)).astype(bf16)
+            eg_ref[r] = (total[...] + mrecv[0, r].astype(jnp.float32)).astype(bf16)
 
         @pl.when(r == blocks - 2)
         def _():
@@ -649,6 +710,7 @@
         @pl.when(is_end)
         def _():
             g_copy(r).wait_send()
+            prod_copy(r).wait_send()
 
         @pl.when(is_inner)
         def _():
@@ -656,11 +718,54 @@
             mid_copy(1, r).wait_send()
             end_copy(r).wait_send()
 
+    for i in range(1, n):
+        back_copy(i).wait_send()
     for i in range(4):
         pair_copy(i).wait_send()
     for way in range(2):
         for i in range(3):
             hop_copy(way, i, hops.at[way, i]).wait_send()
+
+
+def deliver_kernel(table_ref, *refs):
+    count = (len(refs) - 2) // 3
+    ins, outs = refs[:count], refs[count : 2 * count]
+    held, (load_sem, store_sem) = refs[2 * count : 3 * count], refs[3 * count :]
+    loads, stores = [], []
+    for k in range(count):
+        pieces = [(ins[k], held[k], outs[k])]
+        if len(ins[k].shape) == 3:
+            blocks, size, _ = ins[k].shape
+            pieces = [
+                (ins[k].at[table_ref[1, b]], held[k].at[b], outs[k].at[pl.ds(b * size, size), :])
+                for b in range(blocks)
+            ]
+        for source, room, target in pieces:
+            ident = len(loads)
+            load = pltpu.make_async_copy(source, room, load_sem.at[ident])
+            load.start()
+            loads.append(load)
+            stores.append(pltpu.make_async_copy(room, target, store_sem.at[ident]))
+    for load, store in zip(loads, stores):
+        load.wait()
+        store.start()
+    for store in stores:
+        store.wait()
+
+
+def deliver(table, arrays):
+    hbm = pl.BlockSpec(memory_space=pl.ANY)
+    copies = sum(a.shape[0] if a.ndim == 3 else 1 for a in arrays)
+    dma = pltpu.SemaphoreType.DMA((copies,))
+    return pl.pallas_call(
+        deliver_kernel,
+        out_shape=tuple(
+            jax.ShapeDtypeStruct((a.size // a.shape[-1], a.shape[-1]), a.dtype) for a in arrays
+        ),
+        in_specs=[pl.BlockSpec(memory_space=pltpu.SMEM)] + [hbm] * len(arrays),
+        out_specs=(hbm,) * len(arrays),
+        scratch_shapes=[pltpu.VMEM(a.shape, a.dtype) for a in arrays] + [dma, dma],
+    )(table, *arrays)
 
 
 def per_device_cube(
@@ -680,8 +785,14 @@
     tokens = queries.shape[0]
     blocks = rows // BLK
     chips = n // 2
-    hits = block_bin[:, None] == jnp.arange(n, dtype=jnp.int32)[None, :]
-    held = jnp.sum(jnp.where(hits, jnp.arange(blocks, dtype=jnp.int32)[:, None], 0), axis=0)
+    me = lax.axis_index("dp")
+    order = jnp.arange(n, dtype=jnp.int32)
+    hits = block_bin[None, :] == order[:, None]
+    held = jnp.sum(jnp.where(hits, jnp.arange(blocks, dtype=jnp.int32)[None, :], 0), axis=1)
+    hole = (n * (n - 1) // 2 - jnp.sum(block_bin)) ^ me
+    turn = jnp.pad(block_bin, (0, n - blocks)) ^ me
+    turn = jnp.clip(turn - (turn > hole).astype(jnp.int32), 0, blocks - 1)
+    table = jnp.stack([held, turn, (order >= hole).astype(jnp.int32)])
     vmem = pl.BlockSpec(memory_space=pltpu.VMEM)
     smem = pl.BlockSpec(memory_space=pltpu.SMEM)
     hbm = pl.BlockSpec(memory_space=pl.ANY)
@@ -689,14 +800,14 @@
     dma = pltpu.SemaphoreType.DMA
     shape = jax.ShapeDtypeStruct
     pairs = []
-    for extent in [(14,), (8,), (8,), (n,), (n,), (heads, n), (blocks,), (2, blocks), (blocks,), (chips,), (2, 3)]:
+    for extent in [(14,), (8,), (8,), (n,), (heads, n), (n,), (blocks,), (2, blocks), (blocks,), (blocks,), (chips,), (2, 3)]:
         pairs += [dma(extent), dma(extent)]
-    return pl.pallas_call(
+    outs = pl.pallas_call(
         functools.partial(step_kernel, n, count),
         out_shape=(
             shape((tokens, width), bf16),
             shape((tokens, width), bf16),
-            shape((rows, model // count), bf16),
+            shape((blocks, BLK, model // count), bf16),
             shape((depth, width), bf16),
             shape((depth, width), bf16),
         ),
@@ -705,14 +816,15 @@
         scratch_shapes=[
             pltpu.VMEM((rows, model), bf16),
             pltpu.VMEM((n, depth, 2 * width), bf16),
-            pltpu.VMEM((n - 2, depth, 2 * width), bf16),
+            pltpu.VMEM((n // 2, depth, 2 * width), bf16),
             pltpu.VMEM((blocks, BLK, 2 * width), jnp.float32),
-            pltpu.VMEM((n * BLK, 2 * width), bf16),
+            pltpu.VMEM((heads, 2, n * BLK, HD), bf16),
             pltpu.VMEM((n, 8, BLK), jnp.float32),
             pltpu.VMEM((n, 8, BLK), jnp.float32),
-            pltpu.VMEM((n, heads, 2, BLK, HD), bf16),
-            pltpu.VMEM((n, heads, 2, BLK, HD), bf16),
-            pltpu.VMEM((rows, 2 * width), bf16),
+            pltpu.VMEM((heads, 2, n * BLK, HD), bf16),
+            pltpu.VMEM((heads, 2, n * BLK, HD), bf16),
+            pltpu.VMEM((blocks, BLK, 2 * width), bf16),
+            pltpu.VMEM((blocks, BLK, 2 * width), bf16),
             pltpu.VMEM((blocks, BLK, 2 * width), bf16),
             pltpu.VMEM((2, blocks, BLK, 2 * width), bf16),
             pltpu.VMEM((2, blocks, BLK, 2 * width), bf16),
@@ -735,8 +847,9 @@
         document_lengths,
         block_bin,
         block_document,
-        held,
-    )
+        table,
+    )
+    return deliver(table, outs)
 
 
 def solution(mesh):

time: 199 us -> 177 us (0.89); the launches traced: 195 us -> 177 us
  Pallas kernels: 186 us -> 172 us
  local copies, waits for them, and re-layouts: 7.89 us -> 0 us
  other arithmetic: 1.25 us -> 3.34 us
    pallas_call x1, Pallas kernels: 186 us -> 168 us  [per_device_cube(): pl.pallas_call(functools.partial(step_kernel, n, count), out_shape=(shape...]
    unnamed x9 -> x0, local copies, waits for them, and re-layouts: 7.89 us -> none
    pallas_call x0 -> x1, Pallas kernels: none -> 3.73 us  [deliver(): pl.pallas_call(deliver_kernel, out_shape=tuple((jax.ShapeDtypeStruct((a.s...]
where the time goes in v2:
time: 177 us
  Pallas kernels  172 us (97%)
  other arithmetic  3.34 us (2%)
    pallas_call x1, Pallas kernels, per_device_cube(): pl.pallas_call(functools.partial(step_kernel, n, count), out_shape=(shape...  168 us
    pallas_call x1, Pallas kernels, deliver(): pl.pallas_call(deliver_kernel, out_shape=tuple((jax.ShapeDtypeStruct((a.s...  3.73 us

profile of v2, /device:TPU:0, one launch (start us, length us, event | category | flops | bytes accessed | tf_op | source)
XLA Modules:
  0.0 176.5 jit_solution(6015769588188557092)
XLA Ops:
  0.6 1.3 reduce_sum.19
  2.6 0.7 fusion.2
  3.3 0.8 select_reduce_fusion
  4.0 0.6 pad_add_fusion.table_ref
  4.6 168.0 %shard_map.119 = (bf16[256,512]{1,0:T(8,128)(2,1)}, bf16[256,512]{1,0:T(8,128)(2,1)}, bf16[7,128,1024]{2,1,0:T(8,128)(2,1)}, bf16[512,512]{1,0:T(8,128)(2,1)}, bf16[512,512]{1,0:T(8,128)(2,1)}) custom-call(bf16[256,512]{1,0:T(8,128)(2,1)} %q_ref.1, bf16[256,512]{1,0:T(8,128)(2,1)} %g_ref.1, bf16[896,4096]{1,0:T(8,128)(2,1)} %enc_hbm.1, ...), custom_call_target="tpu_custom_call" | custom-call | tf_op jit(solution)/shard_map/pallas_call | solution.py:805
  172.6 3.7 %shard_map.120 = (bf16[256,512]{1,0:T(8,128)(2,1)}, bf16[256,512]{1,0:T(8,128)(2,1)}, bf16[896,1024]{1,0:T(8,128)(2,1)}, bf16[512,512]{1,0:T(8,128)(2,1)}, bf16[512,512]{1,0:T(8,128)(2,1)}) custom-call(s32[3,8]{1,0:T(4,128)} %pad_add_fusion.table_ref, bf16[256,512]{1,0:T(8,128)(2,1)} %get-tuple-element.10.refs_0_, ...), custom_call_target="tpu_custom_call" | custom-call | tf_op jit(solution)/shard_map/pallas_call | solution.py:760
  (1 shorter events, 0.0 us)

commit v3 on v2

--- a/solution.py
+++ b/solution.py
@@ -151,6 +151,29 @@
     )
 
 
+def bin_at(me, i):
+    def flip(bit, turned):
+        return bit + turned - 2 * bit * turned
+
+    core, x, y = me % 2, (me // 2) % 2, me // 4
+    return (flip(y, i // 4) * 2 + flip(x, (i // 2) % 2)) * 2 + flip(core, i % 2)
+
+
+def find(value, options):
+    index = jnp.int32(0)
+    for k, option in enumerate(options):
+        index = jnp.where(option == value, k, index)
+    return index
+
+
+def block_turns(me, n, bins_ref):
+    bins = [bins_ref[b] for b in range(bins_ref.shape[0])]
+    order = [bin_at(me, i) for i in range(n)]
+    hole = find(n * (n - 1) // 2 - sum(bins), order)
+    places = [find(b, order) for b in bins]
+    return hole, [jnp.where(p > hole, p - 1, p) for p in places]
+
+
 def step_kernel(
     n,
     count,
@@ -162,7 +185,6 @@
     lengths_ref,
     bins_ref,
     docs_ref,
-    table_ref,
     ctx_ref,
     qg_ref,
     eg_ref,
@@ -421,12 +443,10 @@
         return pl.ds(pl.multiple_of(slot * blk, blk), blk)
 
     def slot_at(i):
-        flip_c, flip_x, flip_y = i % 2, (i // 2) % 2, i // 4
-        return place(
-            y + flip_y - 2 * y * flip_y,
-            x + flip_x - 2 * x * flip_x,
-            core + flip_c - 2 * core * flip_c,
-        )
+        return bin_at(me, i)
+
+    bins = [bins_ref[b] for b in range(blocks)]
+    hole, turns = block_turns(me, n, bins_ref)
 
     def out_copy(h, i):
         to = slot_at(i)
@@ -441,9 +461,10 @@
     for h in range(heads):
         for i in [*range(1, n), 0]:
             to = slot_at(i)
+            index = find(to, bins)
             for part in range(2):
                 cols = pl.ds(part * width + h * HD, HD)
-                picked = acc[table_ref[0, to], :, cols].astype(bf16)
+                picked = acc[index, :, cols].astype(bf16)
                 if i == 0:
                     arrived[h, part, rows_of(me), :] = picked
                 else:
@@ -511,6 +532,28 @@
     def g_copy(r):
         return remote(own.at[r], gend.at[r], g_send.at[r], g_recv.at[r], mp=mate)
 
+    half = blk // 2
+
+    def half_rows(k):
+        return pl.ds(pl.multiple_of(k * half, half), half)
+
+    def first_g_copy(k):
+        sem = k * blocks
+        return remote(
+            own.at[0, half_rows(k)], gend.at[0, half_rows(k)], g_send.at[sem], g_recv.at[sem], mp=mate
+        )
+
+
+    def first_mid_copy(way, k):
+        sem = k * blocks
+        return remote(
+            msend.at[way, 0, half_rows(k)],
+            mrecv.at[way, 0, half_rows(k)],
+            mid_send.at[way, sem],
+            mid_recv.at[way, sem],
+            mp=across,
+        )
+
     def mid_copy(way, r):
         return remote(
             msend.at[way, r], mrecv.at[way, r], mid_send.at[way, r], mid_recv.at[way, r], mp=across
@@ -544,7 +587,7 @@
             back_recv.at[r + 1],
             dp=at_c,
         ).wait_recv()
-        later = table_ref[2, r] > 0
+        later = hole <= r
         for h in range(heads):
             for part in range(2):
                 own[r, :, pl.ds(part * width + h * HD, HD)] = jnp.where(
@@ -553,7 +596,7 @@
                     ret[h, part, rows_of(slot_at(r)), :],
                 )
 
-        @pl.when(is_end)
+        @pl.when(jnp.logical_and(is_end, r > 0))
         def _():
             g_copy(r).start()
 
@@ -581,7 +624,29 @@
     def half_cols(j):
         return pl.ds(pl.multiple_of(j * width, width), width)
 
-    @pl.loop(0, blocks)
+    collect(0)
+
+    @pl.when(is_end)
+    def _():
+        first_g_copy(0).start()
+        first_g_copy(1).start()
+
+    @pl.when(is_inner)
+    def _():
+        @pl.loop(0, 2)
+        def _(k):
+            first_g_copy(k).wait_recv()
+            for way, dest in ((0, far_end), (1, across)):
+
+                @pl.loop(0, 2)
+                def _(j):
+                    summed = contract(own[0, half_rows(k)], own_weights(dest, j), 1, 1)
+                    summed += contract(gend[0, half_rows(k)], end_weights(dest, j), 1, 1)
+                    msend[way, 0, half_rows(k), half_cols(j)] = summed.astype(bf16)
+
+                first_mid_copy(way, k).start()
+
+    @pl.loop(1, blocks)
     def _(r):
         @pl.when(r < 3)
         def _():
@@ -607,7 +672,7 @@
                 collect(later)
 
             for b in range(blocks):
-                block = own[table_ref[1, b]]
+                block = own[turns[b]]
                 for h in range(heads):
                     for part in range(2):
                         first = part * width + h * HD
@@ -666,6 +731,16 @@
 
     total = acc.at[0]
 
+    def wait_mid(way, r):
+        @pl.when(r == 0)
+        def _():
+            first_mid_copy(way, 0).wait_recv()
+            first_mid_copy(way, 1).wait_recv()
+
+        @pl.when(r > 0)
+        def _():
+            mid_copy(way, r).wait_recv()
+
     def own_product(r, dest):
         @pl.loop(0, 2)
         def _(j):
@@ -676,13 +751,13 @@
         @pl.when(is_inner)
         def _():
             own_product(r, end)
-            mid_copy(0, r).wait_recv()
+            wait_mid(0, r)
             mrecv[0, r] = (total[...] + mrecv[0, r].astype(jnp.float32)).astype(bf16)
             end_copy(r).start()
             own_product(r, z)
             prod_copy(r).wait_recv()
             total[...] += pend[r].astype(jnp.float32)
-            mid_copy(1, r).wait_recv()
+            wait_mid(1, r)
             eg_ref[r] = (total[...] + mrecv[1, r].astype(jnp.float32)).astype(bf16)
 
         @pl.when(is_end)
@@ -709,14 +784,31 @@
     def _(r):
         @pl.when(is_end)
         def _():
-            g_copy(r).wait_send()
             prod_copy(r).wait_send()
 
+            @pl.when(r > 0)
+            def _():
+                g_copy(r).wait_send()
+
         @pl.when(is_inner)
         def _():
-            mid_copy(0, r).wait_send()
-            mid_copy(1, r).wait_send()
             end_copy(r).wait_send()
+
+            @pl.when(r > 0)
+            def _():
+                mid_copy(0, r).wait_send()
+                mid_copy(1, r).wait_send()
+
+    @pl.loop(0, 2)
+    def _(k):
+        @pl.when(is_end)
+        def _():
+            first_g_copy(k).wait_send()
+
+        @pl.when(is_inner)
+        def _():
+            first_mid_copy(0, k).wait_send()
+            first_mid_copy(1, k).wait_send()
 
     for i in range(1, n):
         back_copy(i).wait_send()
@@ -727,7 +819,8 @@
             hop_copy(way, i, hops.at[way, i]).wait_send()
 
 
-def deliver_kernel(table_ref, *refs):
+def deliver_kernel(n, bins_ref, *refs):
+    turns = block_turns(lax.axis_index("dp"), n, bins_ref)[1]
     count = (len(refs) - 2) // 3
     ins, outs = refs[:count], refs[count : 2 * count]
     held, (load_sem, store_sem) = refs[2 * count : 3 * count], refs[3 * count :]
@@ -737,7 +830,7 @@
         if len(ins[k].shape) == 3:
             blocks, size, _ = ins[k].shape
             pieces = [
-                (ins[k].at[table_ref[1, b]], held[k].at[b], outs[k].at[pl.ds(b * size, size), :])
+                (ins[k].at[turns[b]], held[k].at[b], outs[k].at[pl.ds(b * size, size), :])
                 for b in range(blocks)
             ]
         for source, room, target in pieces:
@@ -753,19 +846,19 @@
         store.wait()
 
 
-def deliver(table, arrays):
+def deliver(n, bins, arrays):
     hbm = pl.BlockSpec(memory_space=pl.ANY)
     copies = sum(a.shape[0] if a.ndim == 3 else 1 for a in arrays)
     dma = pltpu.SemaphoreType.DMA((copies,))
     return pl.pallas_call(
-        deliver_kernel,
+        functools.partial(deliver_kernel, n),
         out_shape=tuple(
             jax.ShapeDtypeStruct((a.size // a.shape[-1], a.shape[-1]), a.dtype) for a in arrays
         ),
         in_specs=[pl.BlockSpec(memory_space=pltpu.SMEM)] + [hbm] * len(arrays),
         out_specs=(hbm,) * len(arrays),
         scratch_shapes=[pltpu.VMEM(a.shape, a.dtype) for a in arrays] + [dma, dma],
-    )(table, *arrays)
+    )(bins, *arrays)
 
 
 def per_device_cube(
@@ -785,14 +878,6 @@
     tokens = queries.shape[0]
     blocks = rows // BLK
     chips = n // 2
-    me = lax.axis_index("dp")
-    order = jnp.arange(n, dtype=jnp.int32)
-    hits = block_bin[None, :] == order[:, None]
-    held = jnp.sum(jnp.where(hits, jnp.arange(blocks, dtype=jnp.int32)[None, :], 0), axis=1)
-    hole = (n * (n - 1) // 2 - jnp.sum(block_bin)) ^ me
-    turn = jnp.pad(block_bin, (0, n - blocks)) ^ me
-    turn = jnp.clip(turn - (turn > hole).astype(jnp.int32), 0, blocks - 1)
-    table = jnp.stack([held, turn, (order >= hole).astype(jnp.int32)])
     vmem = pl.BlockSpec(memory_space=pltpu.VMEM)
     smem = pl.BlockSpec(memory_space=pltpu.SMEM)
     hbm = pl.BlockSpec(memory_space=pl.ANY)
@@ -800,7 +885,7 @@
     dma = pltpu.SemaphoreType.DMA
     shape = jax.ShapeDtypeStruct
     pairs = []
-    for extent in [(14,), (8,), (8,), (n,), (heads, n), (n,), (blocks,), (2, blocks), (blocks,), (blocks,), (chips,), (2, 3)]:
+    for extent in [(14,), (8,), (8,), (n,), (heads, n), (n,), (n,), (2, n), (blocks,), (blocks,), (chips,), (2, 3)]:
         pairs += [dma(extent), dma(extent)]
     outs = pl.pallas_call(
         functools.partial(step_kernel, n, count),
@@ -811,7 +896,7 @@
             shape((depth, width), bf16),
             shape((depth, width), bf16),
         ),
-        in_specs=[vmem, vmem, hbm, vmem, vmem, smem, smem, smem, smem],
+        in_specs=[vmem, vmem, hbm, vmem, vmem, smem, smem, smem],
         out_specs=(vmem,) * 5,
         scratch_shapes=[
             pltpu.VMEM((rows, model), bf16),
@@ -847,9 +932,8 @@
         document_lengths,
         block_bin,
         block_document,
-        table,
-    )
-    return deliver(table, outs)
+    )
+    return deliver(n, block_bin, outs)
 
 
 def solution(mesh):

time: 177 us -> 173 us (0.977)
  other arithmetic: 3.34 us -> 0 us
    reduce_sum x2 -> x0, other arithmetic: 2.07 us -> none  [the longest x1 1.29 us: per_device_cube(): hole = n * (n - 1) // 2 - jnp.sum(block_bin) ^ me]
where the time goes in v3:
time: 173 us
  Pallas kernels  172 us (99%)
    pallas_call x1, Pallas kernels, per_device_cube(): pl.pallas_call(functools.partial(step_kernel, n, count), out_shape=(shape...  168 us
    pallas_call x1, Pallas kernels, deliver(): pl.pallas_call(functools.partial(deliver_kernel, n), out_shape=tuple((jax...  3.73 us

profile of v3, /device:TPU:0, one launch (start us, length us, event | category | flops | bytes accessed | tf_op | source)
XLA Modules:
  0.0 172.6 jit_solution(6553736978679643531)
XLA Ops:
  0.6 168.1 %shard_map.119 = (bf16[256,512]{1,0:T(8,128)(2,1)}, bf16[256,512]{1,0:T(8,128)(2,1)}, bf16[7,128,1024]{2,1,0:T(8,128)(2,1)}, bf16[512,512]{1,0:T(8,128)(2,1)}, bf16[512,512]{1,0:T(8,128)(2,1)}) custom-call(bf16[256,512]{1,0:T(8,128)(2,1)} %q_ref.1, bf16[256,512]{1,0:T(8,128)(2,1)} %g_ref.1, bf16[896,4096]{1,0:T(8,128)(2,1)} %enc_hbm.1, ...), custom_call_target="tpu_custom_call" | custom-call | tf_op jit(solution)/shard_map/pallas_call | solution.py:890
  168.7 3.7 %shard_map.120 = (bf16[256,512]{1,0:T(8,128)(2,1)}, bf16[256,512]{1,0:T(8,128)(2,1)}, bf16[896,1024]{1,0:T(8,128)(2,1)}, bf16[512,512]{1,0:T(8,128)(2,1)}, bf16[512,512]{1,0:T(8,128)(2,1)}) custom-call(s32[7]{0:T(128)} %bins_ref.3, bf16[256,512]{1,0:T(8,128)(2,1)} %get-tuple-element.10.refs_0_, bf16[256,512]{1,0:T(8,128)(2,1)} %get-tuple-element.11.refs_1_, ...), custom_call_target="tpu_custom_call" | custom-call | tf_op jit(solution)/shard_map/pallas_call | solution.py:853

commit v4 on v3

--- a/solution.py
+++ b/solution.py
@@ -279,10 +279,12 @@
         pl.semaphore_signal(
             barrier, inc=1, device_id={"dp": (me + d) % n}, device_id_type=MESH
         )
-    for d in range(1, count):
-        pl.semaphore_signal(
-            barrier, inc=1, device_id={"mp": (z + d) % count}, device_id_type=MESH
-        )
+    pl.semaphore_signal(barrier, inc=1, device_id={"mp": mate}, device_id_type=MESH)
+
+    @pl.when(is_inner)
+    def _():
+        pl.semaphore_signal(barrier, inc=1, device_id={"mp": across}, device_id_type=MESH)
+
 
     for d in range(n):
         to = (me + d) % n
@@ -290,81 +292,94 @@
         for b in range(blocks):
             doc = jnp.where(bins_ref[b] == to, docs_ref[b], doc)
         tags[to] = jnp.full(tags.shape[1:], doc.astype(jnp.float32), jnp.float32)
-    pl.semaphore_wait(barrier, n - 1 + count - 1)
+    pl.semaphore_wait(barrier, n + (z + 1) // 2 % 2)
 
     def part_cols(part):
         return pl.ds(part * width, width)
 
-    def land(src, part):
-        return wts.at[src, :, part_cols(part)]
+    def head_cols(part, h):
+        return pl.ds(pl.multiple_of(part * width + h * HD, HD), HD)
+
+    def land(src, part, h):
+        return wts.at[src, :, head_cols(part, h)]
 
     started = []
 
-    def ship(ident, ref, src, part, to):
+    def ship(h, ident, ref, src, part, to):
         copy = remote(
-            ref, land(src, part), gather_send.at[ident], gather_recv.at[ident], dp=to
+            ref, land(src, part, h), gather_send.at[h, ident], gather_recv.at[h, ident], dp=to
         )
         copy.start()
         started.append(copy)
 
-    def landed(ident, src, part):
+    def landed(h, ident, src, part):
         remote(
-            land(src, part), land(src, part), gather_send.at[ident], gather_recv.at[ident], dp=at_c
+            land(src, part, h),
+            land(src, part, h),
+            gather_send.at[h, ident],
+            gather_recv.at[h, ident],
+            dp=at_c,
         ).wait_recv()
 
-    def lifted(src, part):
-        return wend.at[src % 4, :, part_cols(part)]
+    def lifted(src, part, h):
+        return wend.at[src % 4, :, head_cols(part, h)]
 
     ours, theirs = (me, at_x, at_y, at_d), (at_c, c_x, c_y, c_d)
-    pieces = [(0, 0), (0, 1), (1, 0), (2, 1), (1, 1), (2, 0), (3, 0), (3, 1)]
-
-    def lift(i, part, ref=None):
+    early = [(0, 0, 0), (0, 1, 0), (0, 0, 1), (0, 1, 1), (1, 0, 0), (2, 1, 0), (1, 1, 0), (2, 0, 0)]
+    early += [(3, 0, 0), (3, 1, 0), (1, 0, 1), (2, 1, 1), (1, 1, 1), (2, 0, 1)]
+    late = [(3, 0, 1), (3, 1, 1)]
+    pieces = early + late
+
+    def lift(i, part, h, ref=None):
         src = ours[i]
-        ident = 2 * i + part
+        ident = 4 * i + 2 * part + h
 
         @pl.when(jnp.logical_and(is_end, src // 4 != side))
         def _():
             remote(
-                land(src, part) if ref is None else ref,
-                lifted(src, part),
+                land(src, part, h) if ref is None else ref,
+                lifted(src, part, h),
                 lift_send.at[ident],
                 lift_recv.at[ident],
                 mp=mate,
             ).start()
 
     def each_piece(todo, listed, of_end):
-        for i, part in listed:
+        for i, part, h in listed:
 
             @pl.when(jnp.logical_and(is_end if of_end else is_inner, ours[i] // 4 != side))
             def _():
-                todo(i, part, ours[i], theirs[i])
-
-    def lift_copy(i, part, src):
-        ident = 2 * i + part
-        return remote(
-            lifted(src, part), lifted(src, part), lift_send.at[ident], lift_recv.at[ident], mp=mate
-        )
-
-    def core_copy(i, part, src):
-        ident = 2 * i + part
-        return remote(
-            lifted(src, part), lifted(src, part), core_send.at[ident], core_recv.at[ident], dp=at_c
-        )
-
-    def hand_over(i, part, src, mirror):
-        lift_copy(i, part, src).wait_recv()
-        core_copy(i, part, src).start()
-
-    ship(0, kw_ref, me, 0, at_x)
-    ship(3, vw_ref, me, 1, at_y)
-    ship(1, vw_ref, me, 1, at_x)
-    ship(2, kw_ref, me, 0, at_y)
-    ship(6, kw_ref, me, 0, at_c)
-    ship(7, vw_ref, me, 1, at_c)
-    lift(0, 0, kw_ref)
-    lift(0, 1, vw_ref)
-    own_k = pltpu.make_async_copy(kw_ref, land(me, 0), local_sem.at[1])
-    own_v = pltpu.make_async_copy(vw_ref, land(me, 1), local_sem.at[2])
+                todo(i, part, h, ours[i])
+
+    def lift_copy(i, part, h, src):
+        ident = 4 * i + 2 * part + h
+        ref = lifted(src, part, h)
+        return remote(ref, ref, lift_send.at[ident], lift_recv.at[ident], mp=mate)
+
+    def core_copy(i, part, h, src):
+        ident = 4 * i + 2 * part + h
+        ref = lifted(src, part, h)
+        return remote(ref, ref, core_send.at[ident], core_recv.at[ident], dp=at_c)
+
+    def hand_over(i, part, h, src):
+        lift_copy(i, part, h, src).wait_recv()
+        core_copy(i, part, h, src).start()
+
+    def ship_own(h):
+        cols = pl.ds(h * HD, HD)
+        kw, vw = kw_ref.at[:, cols], vw_ref.at[:, cols]
+        ship(h, 0, kw, me, 0, at_x)
+        ship(h, 3, vw, me, 1, at_y)
+        ship(h, 1, vw, me, 1, at_x)
+        ship(h, 2, kw, me, 0, at_y)
+        ship(h, 6, kw, me, 0, at_c)
+        ship(h, 7, vw, me, 1, at_c)
+        lift(0, 0, h, kw)
+        lift(0, 1, h, vw)
+
+    ship_own(0)
+    own_k = pltpu.make_async_copy(kw_ref, wts.at[me, :, part_cols(0)], local_sem.at[1])
+    own_v = pltpu.make_async_copy(vw_ref, wts.at[me, :, part_cols(1)], local_sem.at[2])
     own_k.start()
     own_v.start()
     tag_copies = []
@@ -380,64 +395,58 @@
     own_v.wait()
     load_enc.wait()
 
-    def multiply(src, part, first=False):
-        columns = pl.ds(pl.multiple_of(src * depth, depth), depth)
-
-        @pl.loop(0, width // HD)
+    def multiply(h, first_src, second_src, swap=0, fresh=False):
+        @pl.loop(0, 2)
         def _(t):
-            cols = pl.ds(pl.multiple_of(part * width + t * HD, HD), HD)
+            src = first_src + t * (second_src - first_src)
+            columns = pl.ds(pl.multiple_of(src * depth, depth), depth)
+            cols = head_cols(t + swap - 2 * t * swap, h)
             product = jnp.dot(
                 enc[:, columns], wts[src, :, cols], preferred_element_type=jnp.float32
             ).reshape(blocks, blk, HD)
-            if first:
+            if fresh:
                 acc[:, :, cols] = product
             else:
                 acc[:, :, cols] += product
 
-    multiply(me, 0, True)
-    multiply(me, 1, True)
-    landed(6, at_c, 0)
-    multiply(at_c, 0)
-    landed(7, at_c, 1)
-    multiply(at_c, 1)
-    landed(0, at_x, 0)
-    ship(4, land(at_x, 0), at_x, 0, at_y)
-    ship(8, land(at_x, 0), at_x, 0, at_c)
-    lift(1, 0)
-    landed(3, at_y, 1)
-    ship(5, land(at_y, 1), at_y, 1, at_x)
-    ship(11, land(at_y, 1), at_y, 1, at_c)
-    lift(2, 1)
-    multiply(at_x, 0)
-    multiply(at_y, 1)
-    landed(8, c_x, 0)
-    multiply(c_x, 0)
-    landed(11, c_y, 1)
-    multiply(c_y, 1)
-    landed(1, at_x, 1)
-    ship(9, land(at_x, 1), at_x, 1, at_c)
-    lift(1, 1)
-    landed(2, at_y, 0)
-    ship(10, land(at_y, 0), at_y, 0, at_c)
-    lift(2, 0)
-    multiply(at_x, 1)
-    multiply(at_y, 0)
-    landed(9, c_x, 1)
-    multiply(c_x, 1)
-    landed(10, c_y, 0)
-    multiply(c_y, 0)
-    landed(4, at_d, 0)
-    ship(12, land(at_d, 0), at_d, 0, at_c)
-    lift(3, 0)
-    landed(5, at_d, 1)
-    ship(13, land(at_d, 1), at_d, 1, at_c)
-    lift(3, 1)
-    multiply(at_d, 0)
-    multiply(at_d, 1)
-    landed(12, c_d, 0)
-    multiply(c_d, 0)
-    landed(13, c_d, 1)
-    multiply(c_d, 1)
+    def gather(h, when_passed):
+        multiply(h, me, me, fresh=True)
+        landed(h, 6, at_c, 0)
+        landed(h, 7, at_c, 1)
+        multiply(h, at_c, at_c)
+        landed(h, 0, at_x, 0)
+        ship(h, 4, land(at_x, 0, h), at_x, 0, at_y)
+        ship(h, 8, land(at_x, 0, h), at_x, 0, at_c)
+        lift(1, 0, h)
+        landed(h, 3, at_y, 1)
+        ship(h, 5, land(at_y, 1, h), at_y, 1, at_x)
+        ship(h, 11, land(at_y, 1, h), at_y, 1, at_c)
+        lift(2, 1, h)
+        when_passed()
+        multiply(h, at_x, at_y)
+        landed(h, 8, c_x, 0)
+        landed(h, 11, c_y, 1)
+        multiply(h, c_x, c_y)
+        landed(h, 1, at_x, 1)
+        ship(h, 9, land(at_x, 1, h), at_x, 1, at_c)
+        lift(1, 1, h)
+        landed(h, 2, at_y, 0)
+        ship(h, 10, land(at_y, 0, h), at_y, 0, at_c)
+        lift(2, 0, h)
+        multiply(h, at_y, at_x)
+        landed(h, 9, c_x, 1)
+        landed(h, 10, c_y, 0)
+        multiply(h, c_y, c_x)
+        landed(h, 4, at_d, 0)
+        ship(h, 12, land(at_d, 0, h), at_d, 0, at_c)
+        lift(3, 0, h)
+        landed(h, 5, at_d, 1)
+        ship(h, 13, land(at_d, 1, h), at_d, 1, at_c)
+        lift(3, 1, h)
+        multiply(h, at_d, at_d)
+        landed(h, 12, c_d, 0)
+        landed(h, 13, c_d, 1)
+        multiply(h, c_d, c_d)
 
     def rows_of(slot):
         return pl.ds(pl.multiple_of(slot * blk, blk), blk)
@@ -458,7 +467,7 @@
             dp=to,
         )
 
-    for h in range(heads):
+    def send_slots(h):
         for i in [*range(1, n), 0]:
             to = slot_at(i)
             index = find(to, bins)
@@ -472,7 +481,10 @@
             if i > 0:
                 out_copy(h, i).start()
 
-    each_piece(hand_over, pieces[:6], False)
+    gather(0, lambda: ship_own(1))
+    gather(1, lambda: send_slots(0))
+    send_slots(1)
+    each_piece(hand_over, early, False)
     position = lax.broadcasted_iota(jnp.int32, (tokens, 1), 0)
     token_doc = jnp.zeros(position.shape, jnp.float32)
     doc_end = jnp.int32(0)
@@ -505,7 +517,7 @@
         tsend[h, pl.ds(0, tokens), :] = rounded
         tsend[h, pl.ds(tokens, tokens), :] = score_grad
         if h == 0:
-            each_piece(hand_over, pieces[6:], False)
+            each_piece(hand_over, late, False)
 
     def back_copy(i):
         to = slot_at(i)
@@ -572,11 +584,11 @@
         to = at_x if (way == 0) == (i < 2) else at_y
         return remote(src, hops.at[way, i], hop_send.at[way, i], hop_recv.at[way, i], dp=to)
 
-    for i, part in pieces:
+    for i, part, h in pieces:
 
         @pl.when(jnp.logical_and(is_inner, theirs[i] // 4 != side))
         def _():
-            core_copy(i, part, theirs[i]).wait_recv()
+            core_copy(i, part, h, theirs[i]).wait_recv()
 
     def collect(r):
         back_copy_at = slot_at(r + 1)
@@ -646,6 +658,17 @@
 
                 first_mid_copy(way, k).start()
 
+    def send_across(way, r):
+        dest = across if way else far_end
+
+        @pl.loop(0, 2)
+        def _(j):
+            summed = contract(own[r], own_weights(dest, j), 1, 1)
+            summed += contract(gend[r], end_weights(dest, j), 1, 1)
+            msend[way, r, :, half_cols(j)] = summed.astype(bf16)
+
+        mid_copy(way, r).start()
+
     @pl.loop(1, blocks)
     def _(r):
         @pl.when(r < 3)
@@ -655,15 +678,11 @@
         @pl.when(is_inner)
         def _():
             g_copy(r).wait_recv()
-            for way, dest in ((0, far_end), (1, across)):
-
-                @pl.loop(0, 2)
-                def _(j):
-                    summed = contract(own[r], own_weights(dest, j), 1, 1)
-                    summed += contract(gend[r], end_weights(dest, j), 1, 1)
-                    msend[way, r, :, half_cols(j)] = summed.astype(bf16)
-
-                mid_copy(way, r).start()
+            send_across(0, r)
+
+            @pl.when(r > 1)
+            def _():
+                send_across(1, r - 1)
 
         @pl.when(r == 2)
         def _():
@@ -721,6 +740,10 @@
                 msend[0, r, :, half_cols(j)] = contract(own[r], own_weights(mate, j), 1, 1).astype(bf16)
 
             prod_copy(r).start()
+
+    @pl.when(is_inner)
+    def _():
+        send_across(1, blocks - 1)
 
     for way in range(2):
         hop_copy(way, 1, hops.at[way, 1]).wait_recv()
@@ -777,8 +800,8 @@
 
     for copy in started:
         copy.wait_send()
-    each_piece(lambda i, part, src, mirror: lift_copy(i, part, src).wait_send(), pieces, True)
-    each_piece(lambda i, part, src, mirror: core_copy(i, part, src).wait_send(), pieces, False)
+    each_piece(lambda *piece: lift_copy(*piece).wait_send(), pieces, True)
+    each_piece(lambda *piece: core_copy(*piece).wait_send(), pieces, False)
 
     @pl.loop(0, blocks)
     def _(r):
@@ -885,7 +908,7 @@
     dma = pltpu.SemaphoreType.DMA
     shape = jax.ShapeDtypeStruct
     pairs = []
-    for extent in [(14,), (8,), (8,), (n,), (heads, n), (n,), (n,), (2, n), (blocks,), (blocks,), (chips,), (2, 3)]:
+    for extent in [(heads, 14), (16,), (16,), (n,), (heads, n), (n,), (n,), (2, n), (blocks,), (blocks,), (chips,), (2, 3)]:
         pairs += [dma(extent), dma(extent)]
     outs = pl.pallas_call(
         functools.partial(step_kernel, n, count),

time: 173 us -> 169 us (0.977)
  Pallas kernels: 172 us -> 168 us
    pallas_call x1, Pallas kernels: 168 us -> 164 us  [per_device_cube(): pl.pallas_call(functools.partial(step_kernel, n, count), out_shape=(shape...]
where the time goes in v4:
time: 169 us; the launch traced here: 168 us
  Pallas kernels  168 us (99%)
    pallas_call x1, Pallas kernels, per_device_cube(): pl.pallas_call(functools.partial(step_kernel, n, count), out_shape=(shape...  164 us
    pallas_call x1, Pallas kernels, deliver(): pl.pallas_call(functools.partial(deliver_kernel, n), out_shape=tuple((jax...  3.73 us

profile of v4, /device:TPU:0, one launch (start us, length us, event | category | flops | bytes accessed | tf_op | source)
XLA Modules:
  0.0 168.4 jit_solution(10393788346105031001)
XLA Ops:
  0.6 163.9 %shard_map.119 = (bf16[256,512]{1,0:T(8,128)(2,1)}, bf16[256,512]{1,0:T(8,128)(2,1)}, bf16[7,128,1024]{2,1,0:T(8,128)(2,1)}, bf16[512,512]{1,0:T(8,128)(2,1)}, bf16[512,512]{1,0:T(8,128)(2,1)}) custom-call(bf16[256,512]{1,0:T(8,128)(2,1)} %q_ref.1, bf16[256,512]{1,0:T(8,128)(2,1)} %g_ref.1, bf16[896,4096]{1,0:T(8,128)(2,1)} %enc_hbm.1, ...), custom_call_target="tpu_custom_call" | custom-call | tf_op jit(solution)/shard_map/pallas_call | solution.py:913
  164.5 3.7 %shard_map.120 = (bf16[256,512]{1,0:T(8,128)(2,1)}, bf16[256,512]{1,0:T(8,128)(2,1)}, bf16[896,1024]{1,0:T(8,128)(2,1)}, bf16[512,512]{1,0:T(8,128)(2,1)}, bf16[512,512]{1,0:T(8,128)(2,1)}) custom-call(s32[7]{0:T(128)} %bins_ref.3, bf16[256,512]{1,0:T(8,128)(2,1)} %get-tuple-element.10.refs_0_, bf16[256,512]{1,0:T(8,128)(2,1)} %get-tuple-element.11.refs_1_, ...), custom_call_target="tpu_custom_call" | custom-call | tf_op jit(solution)/shard_map/pallas_call | solution.py:876

commit v5 on v4

--- a/solution.py
+++ b/solution.py
@@ -769,6 +769,13 @@
         def _(j):
             total[:, half_cols(j)] = contract(own[r], own_weights(dest, j), 1, 1)
 
+    def finish(r):
+        own_product(r, z)
+        prod_copy(r).wait_recv()
+        total[...] += pend[r].astype(jnp.float32)
+        wait_mid(1, r)
+        eg_ref[r] = (total[...] + mrecv[1, r].astype(jnp.float32)).astype(bf16)
+
     @pl.loop(0, blocks)
     def _(r):
         @pl.when(is_inner)
@@ -777,11 +784,14 @@
             wait_mid(0, r)
             mrecv[0, r] = (total[...] + mrecv[0, r].astype(jnp.float32)).astype(bf16)
             end_copy(r).start()
-            own_product(r, z)
-            prod_copy(r).wait_recv()
-            total[...] += pend[r].astype(jnp.float32)
-            wait_mid(1, r)
-            eg_ref[r] = (total[...] + mrecv[1, r].astype(jnp.float32)).astype(bf16)
+
+            @pl.when(r > 0)
+            def _():
+                finish(r - 1)
+
+            @pl.when(r == blocks - 1)
+            def _():
+                finish(r)
 
         @pl.when(is_end)
         def _():
@@ -844,43 +854,36 @@
 
 def deliver_kernel(n, bins_ref, *refs):
     turns = block_turns(lax.axis_index("dp"), n, bins_ref)[1]
-    count = (len(refs) - 2) // 3
-    ins, outs = refs[:count], refs[count : 2 * count]
-    held, (load_sem, store_sem) = refs[2 * count : 3 * count], refs[3 * count :]
-    loads, stores = [], []
+    count = (len(refs) - 1) // 2
+    ins, outs, store_sem = refs[:count], refs[count : 2 * count], refs[2 * count]
+    stores = []
     for k in range(count):
-        pieces = [(ins[k], held[k], outs[k])]
+        pieces = [(ins[k], outs[k])]
         if len(ins[k].shape) == 3:
             blocks, size, _ = ins[k].shape
             pieces = [
-                (ins[k].at[turns[b]], held[k].at[b], outs[k].at[pl.ds(b * size, size), :])
-                for b in range(blocks)
+                (ins[k].at[turns[b]], outs[k].at[pl.ds(b * size, size), :]) for b in range(blocks)
             ]
-        for source, room, target in pieces:
-            ident = len(loads)
-            load = pltpu.make_async_copy(source, room, load_sem.at[ident])
-            load.start()
-            loads.append(load)
-            stores.append(pltpu.make_async_copy(room, target, store_sem.at[ident]))
-    for load, store in zip(loads, stores):
-        load.wait()
-        store.start()
+        for source, target in pieces:
+            stores.append(pltpu.make_async_copy(source, target, store_sem.at[len(stores)]))
+            stores[-1].start()
     for store in stores:
         store.wait()
 
 
 def deliver(n, bins, arrays):
     hbm = pl.BlockSpec(memory_space=pl.ANY)
+    vmem = pl.BlockSpec(memory_space=pltpu.VMEM)
     copies = sum(a.shape[0] if a.ndim == 3 else 1 for a in arrays)
-    dma = pltpu.SemaphoreType.DMA((copies,))
     return pl.pallas_call(
         functools.partial(deliver_kernel, n),
         out_shape=tuple(
             jax.ShapeDtypeStruct((a.size // a.shape[-1], a.shape[-1]), a.dtype) for a in arrays
         ),
-        in_specs=[pl.BlockSpec(memory_space=pltpu.SMEM)] + [hbm] * len(arrays),
+        in_specs=[pl.BlockSpec(memory_space=pltpu.SMEM)] + [vmem] * len(arrays),
         out_specs=(hbm,) * len(arrays),
-        scratch_shapes=[pltpu.VMEM(a.shape, a.dtype) for a in arrays] + [dma, dma],
+        scratch_shapes=[pltpu.SemaphoreType.DMA((copies,))],
+        compiler_params=pltpu.CompilerParams(vmem_limit_bytes=8 * 1024 * 1024),
     )(bins, *arrays)
 
 
@@ -906,7 +909,7 @@
     hbm = pl.BlockSpec(memory_space=pl.ANY)
     bf16 = jnp.bfloat16
     dma = pltpu.SemaphoreType.DMA
-    shape = jax.ShapeDtypeStruct
+    shape = pltpu.VMEM
     pairs = []
     for extent in [(heads, 14), (16,), (16,), (n,), (heads, n), (n,), (n,), (2, n), (blocks,), (blocks,), (chips,), (2, 3)]:
         pairs += [dma(extent), dma(extent)]
@@ -944,7 +947,7 @@
             *pairs,
         ],
         compiler_params=pltpu.CompilerParams(
-            collective_id=0, has_side_effects=True, vmem_limit_bytes=67043328
+            collective_id=0, has_side_effects=True, vmem_limit_bytes=60 * 1024 * 1024
         ),
     )(
         queries,

time: 169 us -> 166 us (0.982)
  Pallas kernels: 168 us -> 165 us
    pallas_call x1, Pallas kernels: 164 us -> 162 us  [per_device_cube(): pl.pallas_call(functools.partial(step_kernel, n, count), out_shape=(shape...]
where the time goes in v5:
time: 166 us; the launch traced here: 165 us
  Pallas kernels  165 us (99%)
    pallas_call x1, Pallas kernels, per_device_cube(): pl.pallas_call(functools.partial(step_kernel, n, count), out_shape=(shape...  162 us

profile of v5, /device:TPU:0, one launch (start us, length us, event | category | flops | bytes accessed | tf_op | source)
XLA Modules:
  0.0 165.4 jit_solution(7631733129316427935)
XLA Ops:
  0.6 0.0 copy-start
  0.6 162.2 %shard_map.119 = (bf16[256,512]{1,0:T(8,128)(2,1)S(1)}, bf16[256,512]{1,0:T(8,128)(2,1)S(1)}, bf16[7,128,1024]{2,1,0:T(8,128)(2,1)S(1)}, bf16[512,512]{1,0:T(8,128)(2,1)S(1)}, bf16[512,512]{1,0:T(8,128)(2,1)S(1)}) custom-call(bf16[256,512]{1,0:T(8,128)(2,1)} %q_ref.1, bf16[256,512]{1,0:T(8,128)(2,1)} %g_ref.1, bf16[896,4096]{1,0:T(8,128)(2,1)} %enc_hbm.1, ...), custom_call_target="tpu_custom_call" | custom-call | tf_op jit(solution)/shard_map/pallas_call | solution.py:916
  162.8 0.0 copy-done
  162.8 2.4 %shard_map.120 = (bf16[256,512]{1,0:T(8,128)(2,1)}, bf16[256,512]{1,0:T(8,128)(2,1)}, bf16[896,1024]{1,0:T(8,128)(2,1)}, bf16[512,512]{1,0:T(8,128)(2,1)}, bf16[512,512]{1,0:T(8,128)(2,1)}) custom-call(s32[7]{0:T(128)S(1)} %copy-done, bf16[256,512]{1,0:T(8,128)(2,1)S(1)} %get-tuple-element.10.refs_0_, bf16[256,512]{1,0:T(8,128)(2,1)S(1)} %get-tuple-element.11.refs_1_, ...), custom_call_target="tpu_custom_call" | custom-call | tf_op jit(solution)/shard_map/pallas_call | solution.py:878
Async XLA Ops:
  0.6 162.2 %copy-start = (s32[7]{0:T(128)S(1)}, s32[7]{0:T(128)}, u32[]{:S(2)}) copy-start(s32[7]{0:T(128)} %bins_ref.3) | copy-start | bytes 88

commit v6 on v5

--- a/solution.py
+++ b/solution.py
@@ -636,6 +636,29 @@
     def half_cols(j):
         return pl.ds(pl.multiple_of(j * width, width), width)
 
+    total = acc.at[0]
+
+    def wait_mid(way, r):
+        @pl.when(r == 0)
+        def _():
+            first_mid_copy(way, 0).wait_recv()
+            first_mid_copy(way, 1).wait_recv()
+
+        @pl.when(r > 0)
+        def _():
+            mid_copy(way, r).wait_recv()
+
+    def own_product(r, dest):
+        @pl.loop(0, 2)
+        def _(j):
+            total[:, half_cols(j)] = contract(own[r], own_weights(dest, j), 1, 1)
+
+    def forward(r):
+        own_product(r, end)
+        wait_mid(0, r)
+        mrecv[0, r] = (total[...] + mrecv[0, r].astype(jnp.float32)).astype(bf16)
+        end_copy(r).start()
+
     collect(0)
 
     @pl.when(is_end)
@@ -645,14 +668,21 @@
 
     @pl.when(is_inner)
     def _():
+        crossing = ((0, far_end), (1, across))
+        for way, dest in crossing:
+
+            @pl.loop(0, 2)
+            def _(j):
+                acc[1 + way, :, half_cols(j)] = contract(own[0], own_weights(dest, j), 1, 1)
+
         @pl.loop(0, 2)
         def _(k):
             first_g_copy(k).wait_recv()
-            for way, dest in ((0, far_end), (1, across)):
+            for way, dest in crossing:
 
                 @pl.loop(0, 2)
                 def _(j):
-                    summed = contract(own[0, half_rows(k)], own_weights(dest, j), 1, 1)
+                    summed = acc[1 + way, half_rows(k), half_cols(j)]
                     summed += contract(gend[0, half_rows(k)], end_weights(dest, j), 1, 1)
                     msend[way, 0, half_rows(k), half_cols(j)] = summed.astype(bf16)
 
@@ -683,6 +713,7 @@
             @pl.when(r > 1)
             def _():
                 send_across(1, r - 1)
+                forward(r - 2)
 
         @pl.when(r == 2)
         def _():
@@ -752,23 +783,6 @@
         passed[way] = summed.astype(bf16)
         hop_copy(way, 2, passed.at[way]).start()
 
-    total = acc.at[0]
-
-    def wait_mid(way, r):
-        @pl.when(r == 0)
-        def _():
-            first_mid_copy(way, 0).wait_recv()
-            first_mid_copy(way, 1).wait_recv()
-
-        @pl.when(r > 0)
-        def _():
-            mid_copy(way, r).wait_recv()
-
-    def own_product(r, dest):
-        @pl.loop(0, 2)
-        def _(j):
-            total[:, half_cols(j)] = contract(own[r], own_weights(dest, j), 1, 1)
-
     def finish(r):
         own_product(r, z)
         prod_copy(r).wait_recv()
@@ -780,18 +794,11 @@
     def _(r):
         @pl.when(is_inner)
         def _():
-            own_product(r, end)
-            wait_mid(0, r)
-            mrecv[0, r] = (total[...] + mrecv[0, r].astype(jnp.float32)).astype(bf16)
-            end_copy(r).start()
-
-            @pl.when(r > 0)
+            @pl.when(jnp.logical_and(r + 3 >= blocks, r + 1 < blocks))
             def _():
-                finish(r - 1)
-
-            @pl.when(r == blocks - 1)
-            def _():
-                finish(r)
+                forward(r + 1)
+
+            finish(r)
 
         @pl.when(is_end)
         def _():

time: 166 us -> 157 us (0.946)
  Pallas kernels: 165 us -> 154 us
    pallas_call x1, Pallas kernels: 162 us -> 152 us  [per_device_cube(): pl.pallas_call(functools.partial(step_kernel, n, count), out_shape=(shape...]
where the time goes in v6:
time: 157 us; the launch traced here: 155 us
  Pallas kernels  154 us (98%)
    pallas_call x1, Pallas kernels, per_device_cube(): pl.pallas_call(functools.partial(step_kernel, n, count), out_shape=(shape...  152 us

profile of v6, /device:TPU:0, one launch (start us, length us, event | category | flops | bytes accessed | tf_op | source)
XLA Modules:
  0.0 154.9 jit_solution(14749731427015088476)
XLA Ops:
  0.6 0.0 copy-start
  0.6 151.7 %shard_map.119 = (bf16[256,512]{1,0:T(8,128)(2,1)S(1)}, bf16[256,512]{1,0:T(8,128)(2,1)S(1)}, bf16[7,128,1024]{2,1,0:T(8,128)(2,1)S(1)}, bf16[512,512]{1,0:T(8,128)(2,1)S(1)}, bf16[512,512]{1,0:T(8,128)(2,1)S(1)}) custom-call(bf16[256,512]{1,0:T(8,128)(2,1)} %q_ref.1, bf16[256,512]{1,0:T(8,128)(2,1)} %g_ref.1, bf16[896,4096]{1,0:T(8,128)(2,1)} %enc_hbm.1, ...), custom_call_target="tpu_custom_call" | custom-call | tf_op jit(solution)/shard_map/pallas_call | solution.py:923
  152.3 0.0 copy-done
  152.3 2.4 %shard_map.120 = (bf16[256,512]{1,0:T(8,128)(2,1)}, bf16[256,512]{1,0:T(8,128)(2,1)}, bf16[896,1024]{1,0:T(8,128)(2,1)}, bf16[512,512]{1,0:T(8,128)(2,1)}, bf16[512,512]{1,0:T(8,128)(2,1)}) custom-call(s32[7]{0:T(128)S(1)} %copy-done, bf16[256,512]{1,0:T(8,128)(2,1)S(1)} %get-tuple-element.10.refs_0_, bf16[256,512]{1,0:T(8,128)(2,1)S(1)} %get-tuple-element.11.refs_1_, ...), custom_call_target="tpu_custom_call" | custom-call | tf_op jit(solution)/shard_map/pallas_call | solution.py:885
Async XLA Ops:
  0.6 151.7 %copy-start = (s32[7]{0:T(128)S(1)}, s32[7]{0:T(128)}, u32[]{:S(2)}) copy-start(s32[7]{0:T(128)} %bins_ref.3) | copy-start | bytes 88

commit v7 on v6

--- a/solution.py
+++ b/solution.py
@@ -177,11 +177,11 @@
 def step_kernel(
     n,
     count,
-    q_ref,
-    g_ref,
+    q_hbm,
+    g_hbm,
     enc_hbm,
-    kw_ref,
-    vw_ref,
+    kw_hbm,
+    vw_hbm,
     lengths_ref,
     bins_ref,
     docs_ref,
@@ -190,6 +190,8 @@
     eg_ref,
     kwg_ref,
     vwg_ref,
+    q_ref,
+    g_ref,
     enc,
     wts,
     wend,
@@ -247,7 +249,7 @@
     at_c, at_d = place(y, x, 1 - core), place(1 - y, 1 - x, core)
     c_x, c_y = place(y, 1 - x, 1 - core), place(1 - y, x, 1 - core)
     c_d = place(1 - y, 1 - x, 1 - core)
-    depth, width = kw_ref.shape
+    depth, width = kw_hbm.shape
     rows = enc.shape[0]
     blocks = rows // BLK
     blk = BLK
@@ -272,8 +274,15 @@
             device_id_type=MESH,
         )
 
-    load_enc = pltpu.make_async_copy(enc_hbm, enc, local_sem.at[0])
-    load_enc.start()
+    def load(k, source, target):
+        return pltpu.make_async_copy(source, target, local_sem.at[k])
+
+    own_k = load(1, kw_hbm, wts.at[me, :, pl.ds(0, width)])
+    own_v = load(2, vw_hbm, wts.at[me, :, pl.ds(width, width)])
+    load_enc = load(0, enc_hbm, enc)
+    load_q, load_g = load(3, q_hbm, q_ref), load(4, g_hbm, g_ref)
+    for copy in (own_k, own_v, load_enc, load_q, load_g):
+        copy.start()
     barrier = pltpu.get_barrier_semaphore()
     for d in range(1, n):
         pl.semaphore_signal(
@@ -330,14 +339,14 @@
     late = [(3, 0, 1), (3, 1, 1)]
     pieces = early + late
 
-    def lift(i, part, h, ref=None):
+    def lift(i, part, h):
         src = ours[i]
         ident = 4 * i + 2 * part + h
 
         @pl.when(jnp.logical_and(is_end, src // 4 != side))
         def _():
             remote(
-                land(src, part, h) if ref is None else ref,
+                land(src, part, h),
                 lifted(src, part, h),
                 lift_send.at[ident],
                 lift_recv.at[ident],
@@ -366,22 +375,19 @@
         core_copy(i, part, h, src).start()
 
     def ship_own(h):
-        cols = pl.ds(h * HD, HD)
-        kw, vw = kw_ref.at[:, cols], vw_ref.at[:, cols]
+        kw, vw = land(me, 0, h), land(me, 1, h)
         ship(h, 0, kw, me, 0, at_x)
         ship(h, 3, vw, me, 1, at_y)
         ship(h, 1, vw, me, 1, at_x)
         ship(h, 2, kw, me, 0, at_y)
         ship(h, 6, kw, me, 0, at_c)
         ship(h, 7, vw, me, 1, at_c)
-        lift(0, 0, h, kw)
-        lift(0, 1, h, vw)
-
+        lift(0, 0, h)
+        lift(0, 1, h)
+
+    own_k.wait()
+    own_v.wait()
     ship_own(0)
-    own_k = pltpu.make_async_copy(kw_ref, wts.at[me, :, part_cols(0)], local_sem.at[1])
-    own_v = pltpu.make_async_copy(vw_ref, wts.at[me, :, part_cols(1)], local_sem.at[2])
-    own_k.start()
-    own_v.start()
     tag_copies = []
     for d in range(1, n):
         to = (me + d) % n
@@ -391,8 +397,6 @@
         copy.start()
         tag_copies.append(copy)
     arrived_tags[me] = tags[me]
-    own_k.wait()
-    own_v.wait()
     load_enc.wait()
 
     def multiply(h, first_src, second_src, swap=0, fresh=False):
@@ -493,6 +497,8 @@
         token_doc = token_doc + jnp.where(position >= doc_end, 1.0, 0.0)
     for copy in tag_copies:
         copy.wait()
+    load_q.wait()
+    load_g.wait()
     tag_row = jnp.concatenate([arrived_tags[s, 0:1, :] for s in range(n)], axis=1)
     live = tag_row == token_doc
     present = jnp.max(jnp.where(live, 1.0, 0.0), axis=1, keepdims=True) > 0.0
@@ -532,35 +538,27 @@
     for i in range(1, n):
         back_copy(i).start()
     ret[:, :, rows_of(me), :] = grads[:, :, rows_of(me), :]
-    for h in range(heads):
-        hk = pl.ds(h * HD, HD)
-        ctx_ref[:, hk] = jnp.dot(
-            tsend[h, pl.ds(0, tokens), :], arrived[h, 1], preferred_element_type=jnp.float32
-        ).astype(bf16)
-        qg_ref[:, hk] = jnp.dot(
-            tsend[h, pl.ds(tokens, tokens), :], arrived[h, 0], preferred_element_type=jnp.float32
-        ).astype(bf16)
-
     def g_copy(r):
         return remote(own.at[r], gend.at[r], g_send.at[r], g_recv.at[r], mp=mate)
 
-    half = blk // 2
-
-    def half_rows(k):
-        return pl.ds(pl.multiple_of(k * half, half), half)
+    pieces_first = 4
+    piece = blk // pieces_first
+
+    def piece_rows(k):
+        return pl.ds(pl.multiple_of(k * piece, piece), piece)
 
     def first_g_copy(k):
-        sem = k * blocks
+        sem = blocks + k
         return remote(
-            own.at[0, half_rows(k)], gend.at[0, half_rows(k)], g_send.at[sem], g_recv.at[sem], mp=mate
+            own.at[0, piece_rows(k)], gend.at[0, piece_rows(k)], g_send.at[sem], g_recv.at[sem], mp=mate
         )
 
 
     def first_mid_copy(way, k):
-        sem = k * blocks
+        sem = blocks + k
         return remote(
-            msend.at[way, 0, half_rows(k)],
-            mrecv.at[way, 0, half_rows(k)],
+            msend.at[way, 0, piece_rows(k)],
+            mrecv.at[way, 0, piece_rows(k)],
             mid_send.at[way, sem],
             mid_recv.at[way, sem],
             mp=across,
@@ -641,8 +639,9 @@
     def wait_mid(way, r):
         @pl.when(r == 0)
         def _():
-            first_mid_copy(way, 0).wait_recv()
-            first_mid_copy(way, 1).wait_recv()
+            @pl.loop(0, pieces_first)
+            def _(k):
+                first_mid_copy(way, k).wait_recv()
 
         @pl.when(r > 0)
         def _():
@@ -663,8 +662,18 @@
 
     @pl.when(is_end)
     def _():
-        first_g_copy(0).start()
-        first_g_copy(1).start()
+        @pl.loop(0, pieces_first)
+        def _(k):
+            first_g_copy(k).start()
+
+    for h in range(heads):
+        hk = pl.ds(h * HD, HD)
+        ctx_ref[:, hk] = jnp.dot(
+            tsend[h, pl.ds(0, tokens), :], arrived[h, 1], preferred_element_type=jnp.float32
+        ).astype(bf16)
+        qg_ref[:, hk] = jnp.dot(
+            tsend[h, pl.ds(tokens, tokens), :], arrived[h, 0], preferred_element_type=jnp.float32
+        ).astype(bf16)
 
     @pl.when(is_inner)
     def _():
@@ -675,16 +684,16 @@
             def _(j):
                 acc[1 + way, :, half_cols(j)] = contract(own[0], own_weights(dest, j), 1, 1)
 
-        @pl.loop(0, 2)
+        @pl.loop(0, pieces_first)
         def _(k):
             first_g_copy(k).wait_recv()
             for way, dest in crossing:
 
                 @pl.loop(0, 2)
                 def _(j):
-                    summed = acc[1 + way, half_rows(k), half_cols(j)]
-                    summed += contract(gend[0, half_rows(k)], end_weights(dest, j), 1, 1)
-                    msend[way, 0, half_rows(k), half_cols(j)] = summed.astype(bf16)
+                    summed = acc[1 + way, piece_rows(k), half_cols(j)]
+                    summed += contract(gend[0, piece_rows(k)], end_weights(dest, j), 1, 1)
+                    msend[way, 0, piece_rows(k), half_cols(j)] = summed.astype(bf16)
 
                 first_mid_copy(way, k).start()
 
@@ -839,7 +848,7 @@
                 mid_copy(0, r).wait_send()
                 mid_copy(1, r).wait_send()
 
-    @pl.loop(0, 2)
+    @pl.loop(0, pieces_first)
     def _(k):
         @pl.when(is_end)
         def _():
@@ -918,7 +927,7 @@
     dma = pltpu.SemaphoreType.DMA
     shape = pltpu.VMEM
     pairs = []
-    for extent in [(heads, 14), (16,), (16,), (n,), (heads, n), (n,), (n,), (2, n), (blocks,), (blocks,), (chips,), (2, 3)]:
+    for extent in [(heads, 14), (16,), (16,), (n,), (heads, n), (n,), (blocks + 4,), (2, blocks + 4), (blocks,), (blocks,), (chips,), (2, 3)]:
         pairs += [dma(extent), dma(extent)]
     outs = pl.pallas_call(
         functools.partial(step_kernel, n, count),
@@ -929,9 +938,11 @@
             shape((depth, width), bf16),
             shape((depth, width), bf16),
         ),
-        in_specs=[vmem, vmem, hbm, vmem, vmem, smem, smem, smem],
+        in_specs=[hbm, hbm, hbm, hbm, hbm, smem, smem, smem],
         out_specs=(vmem,) * 5,
         scratch_shapes=[
+            pltpu.VMEM((tokens, width), bf16),
+            pltpu.VMEM((tokens, width), bf16),
             pltpu.VMEM((rows, model), bf16),
             pltpu.VMEM((n, depth, 2 * width), bf16),
             pltpu.VMEM((n // 2, depth, 2 * width), bf16),
@@ -950,7 +961,7 @@
             pltpu.VMEM((chips, depth, 2 * width), bf16),
             pltpu.VMEM((2, 3, depth, width), bf16),
             pltpu.VMEM((2, depth, width), bf16),
-            dma((3,)),
+            dma((5,)),
             *pairs,
         ],
         compiler_params=pltpu.CompilerParams(

time: 157 us -> 156 us (level)
  no operation moved by 1% of the time
where the time goes in v7:
time: 156 us; the launch traced here: 154 us
  Pallas kernels  153 us (98%)
    pallas_call x1, Pallas kernels, per_device_cube(): pl.pallas_call(functools.partial(step_kernel, n, count), out_shape=(shape...  150 us

profile of v7, /device:TPU:0, one launch (start us, length us, event | category | flops | bytes accessed | tf_op | source)
XLA Modules:
  0.0 153.6 jit_solution(9116085662951070999)
XLA Ops:
  0.6 0.0 copy-start
  0.6 150.4 %shard_map.119 = (bf16[256,512]{1,0:T(8,128)(2,1)S(1)}, bf16[256,512]{1,0:T(8,128)(2,1)S(1)}, bf16[7,128,1024]{2,1,0:T(8,128)(2,1)S(1)}, bf16[512,512]{1,0:T(8,128)(2,1)S(1)}, bf16[512,512]{1,0:T(8,128)(2,1)S(1)}) custom-call(bf16[256,512]{1,0:T(8,128)(2,1)} %q_hbm.1, bf16[256,512]{1,0:T(8,128)(2,1)} %g_hbm.1, bf16[896,4096]{1,0:T(8,128)(2,1)} %enc_hbm.1, ...), custom_call_target="tpu_custom_call" | custom-call | tf_op jit(solution)/shard_map/pallas_call | solution.py:932
  151.0 0.0 copy-done
  151.0 2.4 %shard_map.120 = (bf16[256,512]{1,0:T(8,128)(2,1)}, bf16[256,512]{1,0:T(8,128)(2,1)}, bf16[896,1024]{1,0:T(8,128)(2,1)}, bf16[512,512]{1,0:T(8,128)(2,1)}, bf16[512,512]{1,0:T(8,128)(2,1)}) custom-call(s32[7]{0:T(128)S(1)} %copy-done, bf16[256,512]{1,0:T(8,128)(2,1)S(1)} %get-tuple-element.10.refs_0_, bf16[256,512]{1,0:T(8,128)(2,1)S(1)} %get-tuple-element.11.refs_1_, ...), custom_call_target="tpu_custom_call" | custom-call | tf_op jit(solution)/shard_map/pallas_call | solution.py:894
Async XLA Ops:
  0.6 150.4 %copy-start = (s32[7]{0:T(128)S(1)}, s32[7]{0:T(128)}, u32[]{:S(2)}) copy-start(s32[7]{0:T(128)} %bins_ref.3) | copy-start | bytes 88

commit v8 on v7

--- a/solution.py
+++ b/solution.py
@@ -461,29 +461,27 @@
     bins = [bins_ref[b] for b in range(blocks)]
     hole, turns = block_turns(me, n, bins_ref)
 
-    def out_copy(h, i):
+    def out_copy(h, part, i):
         to = slot_at(i)
         return remote(
-            grads.at[h, :, rows_of(to), :],
-            arrived.at[h, :, rows_of(me), :],
-            out_send.at[h, i],
-            out_recv.at[h, i],
+            grads.at[h, part, rows_of(to), :],
+            arrived.at[h, part, rows_of(me), :],
+            out_send.at[h, part, i],
+            out_recv.at[h, part, i],
             dp=to,
         )
 
     def send_slots(h):
-        for i in [*range(1, n), 0]:
-            to = slot_at(i)
-            index = find(to, bins)
-            for part in range(2):
-                cols = pl.ds(part * width + h * HD, HD)
-                picked = acc[index, :, cols].astype(bf16)
+        for part in range(2):
+            cols = pl.ds(part * width + h * HD, HD)
+            for i in [*range(1, n), 0]:
+                to = slot_at(i)
+                picked = acc[find(to, bins), :, cols].astype(bf16)
                 if i == 0:
                     arrived[h, part, rows_of(me), :] = picked
                 else:
                     grads[h, part, rows_of(to), :] = picked
-            if i > 0:
-                out_copy(h, i).start()
+                    out_copy(h, part, i).start()
 
     gather(0, lambda: ship_own(1))
     gather(1, lambda: send_slots(0))
@@ -505,7 +503,7 @@
     scaling = HD ** (-0.5)
     for h in range(heads):
         for i in range(1, n):
-            out_copy(h, i).wait()
+            out_copy(h, 0, i).wait()
         hk = pl.ds(h * HD, HD)
         q, g = q_ref[:, hk], g_ref[:, hk]
         scores = contract(q, arrived[h, 0], 1, 1) * scaling
@@ -515,6 +513,8 @@
         totals = jnp.maximum(jnp.sum(raised, axis=1, keepdims=True), 1.0)
         attention = raised / totals
         rounded = attention.astype(bf16)
+        for i in range(1, n):
+            out_copy(h, 1, i).wait()
         grad_raw = contract(g, arrived[h, 1], 1, 1)
         deltas = jnp.sum(attention * grad_raw, axis=1, keepdims=True)
         score_grad = (attention * (grad_raw - deltas) * scaling).astype(bf16)
@@ -927,7 +927,7 @@
     dma = pltpu.SemaphoreType.DMA
     shape = pltpu.VMEM
     pairs = []
-    for extent in [(heads, 14), (16,), (16,), (n,), (heads, n), (n,), (blocks + 4,), (2, blocks + 4), (blocks,), (blocks,), (chips,), (2, 3)]:
+    for extent in [(heads, 14), (16,), (16,), (n,), (heads, 2, n), (n,), (blocks + 4,), (2, blocks + 4), (blocks,), (blocks,), (chips,), (2, 3)]:
         pairs += [dma(extent), dma(extent)]
     outs = pl.pallas_call(
         functools.partial(step_kernel, n, count),

time: 156 us -> 156 us (level)
  no operation moved by 1% of the time
where the time goes in v8:
time: 156 us; the launch traced here: 154 us
  Pallas kernels  153 us (98%)
    pallas_call x1, Pallas kernels, per_device_cube(): pl.pallas_call(functools.partial(step_kernel, n, count), out_shape=(shape...  150 us

profile of v8, /device:TPU:0, one launch (start us, length us, event | category | flops | bytes accessed | tf_op | source)
XLA Modules:
  0.0 153.5 jit_solution(9171805317697176250)
XLA Ops:
  0.6 0.0 copy-start
  0.6 150.3 %shard_map.119 = (bf16[256,512]{1,0:T(8,128)(2,1)S(1)}, bf16[256,512]{1,0:T(8,128)(2,1)S(1)}, bf16[7,128,1024]{2,1,0:T(8,128)(2,1)S(1)}, bf16[512,512]{1,0:T(8,128)(2,1)S(1)}, bf16[512,512]{1,0:T(8,128)(2,1)S(1)}) custom-call(bf16[256,512]{1,0:T(8,128)(2,1)} %q_hbm.1, bf16[256,512]{1,0:T(8,128)(2,1)} %g_hbm.1, bf16[896,4096]{1,0:T(8,128)(2,1)} %enc_hbm.1, ...), custom_call_target="tpu_custom_call" | custom-call | tf_op jit(solution)/shard_map/pallas_call | solution.py:932
  151.0 0.0 copy-done
  151.0 2.4 %shard_map.120 = (bf16[256,512]{1,0:T(8,128)(2,1)}, bf16[256,512]{1,0:T(8,128)(2,1)}, bf16[896,1024]{1,0:T(8,128)(2,1)}, bf16[512,512]{1,0:T(8,128)(2,1)}, bf16[512,512]{1,0:T(8,128)(2,1)}) custom-call(s32[7]{0:T(128)S(1)} %copy-done, bf16[256,512]{1,0:T(8,128)(2,1)S(1)} %get-tuple-element.10.refs_0_, bf16[256,512]{1,0:T(8,128)(2,1)S(1)} %get-tuple-element.11.refs_1_, ...), custom_call_target="tpu_custom_call" | custom-call | tf_op jit(solution)/shard_map/pallas_call | solution.py:894
Async XLA Ops:
  0.6 150.4 %copy-start = (s32[7]{0:T(128)S(1)}, s32[7]{0:T(128)}, u32[]{:S(2)}) copy-start(s32[7]{0:T(128)} %bins_ref.3) | copy-start | bytes 88
